TPU v7x, 32 devices: a whole 2x2x4 slice. The times are simulated.
32 devices in a mesh: px: 2 (over y), py: 4 (over z), case: 4 (over x, core).
Axes of the slice: x: 2, y: 2, z: 4, core: 2. Of those that a mesh axis runs over, the one named last changes fastest.
Arguments:
- comp_type: int32 [1024], P(('px', 'py')), may hold values from 0 to 7
- stiffness: float32 [1024], P(('px', 'py')), may hold values from 0.3 to 3
- near_port: int32 [1024], P(('px', 'py')), may hold values from 0 to 127
- far_owner: int32 [1024, 1], P(('px', 'py')), may hold values from 0 to 7; in each aligned block of 128 rows (0 to 127, 128 to 255, ...) at most 24 rows name the same one
- far_port: int32 [1024], P(('px', 'py')), may hold values from 0 to 127
- bubble_load: float32 [64, 32, 1024], P(None, 'case', ('px', 'py')), may hold values from -6 to 6
- port_load: float32 [48, 32, 1024], P(None, 'case', ('px', 'py')), may hold values from -3 to 3
- bubble_inverse: float32 [8, 64, 64], replicated, may hold values from -1.5 to 2, as said below
- coupling: float32 [8, 96, 64], replicated, may hold values from -0.1 to 0.1
- port_block: float32 [8, 96, 96], replicated, may hold values from -3 to 8, as said below
Outputs:
- port_solution: float32 [48, 32, 1024], P(None, 'case', ('px', 'py'))
- port_residual: float32 [48, 32, 1024], P(None, 'case', ('px', 'py'))
- bubble_solution: float32 [64, 32, 1024], P(None, 'case', ('px', 'py'))
Inputs may be any that keep to these rules, and one draw needn't show every extreme that they name: `far_owner`: among the 128 components of one partition, at most 24 name the same owner, a bound that some block reaches. `bubble_inverse`: each matrix is symmetric positive definite. `port_block`: each matrix is symmetric positive definite.
All inputs are finite; a program needn't handle non-finite values.
Results may differ from a plain program's by a relative error of at most 0.00016.
Values sent between devices are 32-bit elements; how exact they have to be, the bound alone decides.
A program may use at most 64 MiB of HBM per device.

v0:
```python
import jax
import jax.numpy as jnp
from jax import lax
from jax.experimental import pallas as pl
from jax.experimental.pallas import tpu as pltpu
from jax.sharding import PartitionSpec as P

HIGH = lax.Precision.HIGHEST
F32 = jnp.float32
BF16 = jnp.bfloat16
MESH = pl.DeviceIdType.MESH
NT = (((1,), (1,)), ((), ()))
TN = (((0,), (0,)), ((), ()))


def split(x):
    top = x.astype(BF16)
    return top, (x - top.astype(F32)).astype(BF16)


def mm(a, b):
    return jnp.dot(a, b, preferred_element_type=F32)


def exact(a, b, dims=(((1,), (0,)), ((), ()))):
    return lax.dot_general(a, b, dims, precision=HIGH, preferred_element_type=F32)


def gauss_solve(matrix, target):
    n = matrix.shape[0]
    aug = jnp.concatenate([matrix, target], axis=1)
    rows = lax.broadcasted_iota(jnp.int32, aug.shape, 0)
    for j in range(n):
        row = aug[j:j + 1, :]
        row = row / row[:, j:j + 1]
        aug = jnp.where(rows == j, row, aug - aug[:, j:j + 1] * row)
    return aug[:, n:]


def kernel(
    sizes,
    idx_ref,
    stiff_ref,
    bload_ref,
    pload_ref,
    binv_ref,
    coup_ref,
    pblock_ref,
    sol_ref,
    res_ref,
    bub_ref,
    ask_send,
    ask_recv,
    far_send,
    far_recv,
    nat,
    gath,
    rows_all,
    pair_send,
    pair_recv,
    last_send,
    last_recv,
    inv_keep,
    nat_far,
    part_ssem,
    part_rsem,
    case_ssem,
    case_rsem,
):
    gram_refs = ((pair_send, pair_recv), (last_send, last_recv))
    parts, npy, nq, depth, width, chunks = sizes
    kinds = binv_ref.shape[0]
    modes, ncase, ncomp = bload_ref.shape
    pd = pload_ref.shape[0]
    nport = pload_ref.shape[2]
    slots = parts * depth
    allcase = nq * ncase
    my_x, my_y, my_c = lax.axis_index("px"), lax.axis_index("py"), lax.axis_index("case")
    me = my_x * npy + my_y

    def part_id(step):
        other = lax.rem(me + step + parts, parts)
        return (other // npy, lax.rem(other, npy), my_c)

    def case_id(step):
        if nq == 4:
            other = my_c + (step % 2) * (1 - 2 * lax.rem(my_c, 2))
            other = other + (step // 2) * (2 - 4 * (my_c // 2))
        else:
            other = lax.rem(my_c + step, nq)
        return (my_x, my_y, other)

    direct = (1, 2) if nq == 4 else tuple(range(1, nq))

    barrier = pltpu.get_barrier_semaphore()

    def greet_part(i, _):
        pl.semaphore_signal(barrier, inc=1, device_id=part_id(i), device_id_type=MESH)
        return 0

    lax.fori_loop(1, parts, greet_part, 0)
    for i in range(1, nq):
        pl.semaphore_signal(barrier, inc=1, device_id=case_id(i), device_id_type=MESH)

    kind_row = idx_ref[0:1, :]
    near_row = idx_ref[1:2, :]
    owner_row = idx_ref[2:3, :]
    far_row = idx_ref[3:4, :]

    def as_column(row):
        return jnp.broadcast_to(row.astype(F32), (ncomp, ncomp)).T

    sub = lax.broadcasted_iota(jnp.int32, (ncomp, ncomp), 0)
    lane = lax.broadcasted_iota(jnp.int32, (ncomp, ncomp), 1)
    same = (as_column(owner_row) == owner_row.astype(F32)) & (sub < lane)
    rank = jnp.sum(jnp.where(same, 1.0, 0.0), axis=0, keepdims=True).astype(jnp.int32)
    slot_row = lax.rem(owner_row - me + parts, parts) * depth + rank
    slot_sub = lax.broadcasted_iota(jnp.int32, (slots, ncomp), 0)
    slot_f = jnp.where(slot_sub == slot_row, 1.0, 0.0)
    slot_pick = slot_f.astype(BF16)
    wanted = jnp.sum(slot_f * (far_row + 1).astype(F32), axis=1, keepdims=True) - 1.0
    wanted = jnp.broadcast_to(wanted, (slots, nport)).reshape(parts, depth, nport)
    ask_send[...] = wanted
    ask_recv[0] = wanted[0]
    near_in = jnp.where(sub == near_row, 1.0, 0.0).astype(BF16)
    near_out = jnp.where(lane.astype(F32) == as_column(near_row), 1.0, 0.0).astype(BF16)

    pl.semaphore_wait(barrier, parts - 1 + nq - 1)

    def send_parts(src, dst, e, sign):
        def body(i, _):
            pltpu.make_async_remote_copy(
                src_ref=src(i),
                dst_ref=dst(i),
                send_sem=part_ssem.at[e],
                recv_sem=part_rsem.at[e],
                device_id=part_id(i if sign > 0 else -i),
                device_id_type=MESH,
            ).start()
            return 0

        if parts <= 8:
            for i in range(1, parts):
                body(i, 0)
        else:
            lax.fori_loop(1, parts, body, 0)

    def wait_on(ref, sem):
        pltpu.make_async_copy(ref, ref, sem).wait()

    rest = pl.ds(1, parts - 1)
    send_parts(lambda i: ask_send.at[i], lambda i: ask_recv.at[i], 0, 1)

    inv_tab = split(jnp.concatenate([binv_ref[t] for t in range(kinds)], axis=1))
    coup_tab = split(jnp.concatenate([coup_ref[t].T for t in range(kinds)], axis=1))

    def tile_cases(row):
        return jnp.concatenate([row] * ncase, axis=1)

    stiff = tile_cases(stiff_ref[...])
    kind_all = tile_cases(kind_row)
    masks = [jnp.where(kind_all == t, 1.0, 0.0).astype(BF16) for t in range(kinds)]

    def apply_tables(tab, x):
        top, low = split(x)
        lanes = x.shape[1]
        xt = jnp.concatenate([top * m[:, :lanes] for m in masks], axis=0)
        xl = jnp.concatenate([low * m[:, :lanes] for m in masks], axis=0)
        return mm(tab[0], xt) + mm(tab[0], xl) + mm(tab[1], xt)

    def wide(field, rows):
        return jnp.concatenate(
            [field[k * rows:(k + 1) * rows] for k in range(field.shape[0] // rows)], axis=1
        )

    def tall(x):
        return jnp.concatenate(
            [x[:, k * ncomp:(k + 1) * ncomp] for k in range(x.shape[1] // ncomp)], axis=0
        )

    def pick(x, onehot):
        top, low = split(x)
        return mm(jnp.concatenate([top, low], axis=1), jnp.concatenate([onehot, onehot], axis=0))

    def start_far(e, j, onehot, x, sign):
        top, low = split(x)
        out = lax.dot_general(
            jnp.concatenate([onehot, onehot], axis=1),
            jnp.concatenate([top, low], axis=1),
            NT,
            preferred_element_type=F32,
        ).reshape(parts, depth, width)
        far_send[e, j] = out
        far_recv[e, j, 0] = out[0]
        send_parts(
            lambda i: far_send.at[e, j, i], lambda i: far_recv.at[e, j, i], 3 + e * chunks + j, sign
        )

    def finish_far(e, j, onehot):
        wait_on(far_recv.at[e, j, rest], part_rsem.at[3 + e * chunks + j])
        got = far_recv[e, j].reshape(slots, width).T
        top, low = split(got)
        return mm(top, onehot) + mm(low, onehot)

    def send_case(f, src, block, step):
        pltpu.make_async_remote_copy(
            src_ref=src,
            dst_ref=gath.at[f, block],
            send_sem=case_ssem.at[f, block],
            recv_sem=case_rsem.at[f, block],
            device_id=case_id(step),
            device_id_type=MESH,
        ).start()

    def publish(f, field):
        for k in range(ncase):
            nat[f, :, k, :] = field[k * pd:(k + 1) * pd]
        for i in reversed(direct):
            send_case(f, nat.at[f], i, i)

    def forward(f):
        if nq == 4:
            wait_on(gath.at[f, 2], case_rsem.at[f, 2])
            send_case(f, gath.at[f, 2], 3, 1)

    def collect(f):
        for i in range(1, nq):
            if nq != 4 or i != 2:
                wait_on(gath.at[f, i], case_rsem.at[f, i])

        def body(d, _):
            cols = pl.ds(pl.multiple_of(d * nport, nport), nport)
            rows_all[pl.ds(f * allcase, ncase), cols] = nat[f, d]
            for q in range(1, nq):
                rows_all[pl.ds(f * allcase + q * ncase, ncase), cols] = gath[f, q, d]
            return 0

        lax.fori_loop(0, pd, body, 0, unroll=4)

    def start_gram(s, value):
        sent, got = gram_refs[s]
        folded = jnp.concatenate(
            [value[8 * r:8 * r + 8] for r in range(value.shape[0] // 8)], axis=1
        )
        sent[...] = folded
        got[0] = folded
        send_parts(lambda i: sent, lambda i: got.at[i], 1 + s, 1)

    def finish_gram(s):
        got = gram_refs[s][1]
        wait_on(got.at[rest], part_rsem.at[1 + s])
        total = jnp.sum(got[...], axis=0)
        return jnp.concatenate(
            [total[:, allcase * r:allcase * (r + 1)] for r in range(total.shape[1] // allcase)],
            axis=0,
        )

    def sym(g):
        return 0.5 * (g + g.T)

    def part(x, j):
        return x[j * width:(j + 1) * width]

    loads = jnp.concatenate([bload_ref[:, k, :] for k in range(ncase)], axis=1)
    lifted = apply_tables(inv_tab, loads)
    inv_keep[...] = lifted
    condensed = -apply_tables(coup_tab, lifted)
    leaving = tall(condensed[pd:])
    for j in range(chunks):
        start_far(0, j, slot_pick, part(leaving, j), 1)
    red_t = [exact(binv_ref[t], coup_ref[t], TN) for t in range(kinds)]
    schur = [pblock_ref[t] - exact(red_t[t], coup_ref[t], TN) for t in range(kinds)]
    schur_tab = split(jnp.concatenate(schur, axis=1))
    red_tab = split(jnp.concatenate(red_t, axis=1))
    own = jnp.concatenate([pload_ref[:, k, :] for k in range(ncase)], axis=0)
    own = own + pick(tall(condensed[:pd]), near_out)
    wait_on(ask_recv.at[rest], part_rsem.at[0])
    port_lane = lax.broadcasted_iota(jnp.int32, (slots, nport), 1).astype(F32)
    asked_pick = jnp.where(ask_recv[...].reshape(slots, nport) == port_lane, 1.0, 0.0).astype(BF16)

    def arrive(e, own, onward):
        pieces = []
        for j in range(chunks):
            piece = part(own, j) + finish_far(e, j, asked_pick)
            if onward:
                start_far(e + 1, j, asked_pick, piece, -1)
            pieces.append(piece)
        return jnp.concatenate(pieces, axis=0)

    def operate(e, near):
        cuts = [0, ((chunks - 1) * width) // pd, ncase] if chunks > 1 else [0, ncase]
        far, near_y, far_y, sent, have = None, None, None, 0, 0
        for a, b in zip(cuts[:-1], cuts[1:]):
            while have * width < b * pd:
                piece = finish_far(e, have, slot_pick)
                far = piece if far is None else jnp.concatenate([far, piece], axis=0)
                have += 1
            rows = slice(a * pd, b * pd)
            ends = jnp.concatenate([wide(near[rows], pd), wide(far[rows], pd)], axis=0)
            y = apply_tables(schur_tab, ends) * stiff[:, a * ncomp:b * ncomp]
            out = tall(y[pd:])
            far_y = out if far_y is None else jnp.concatenate([far_y, out], axis=0)
            out = tall(y[:pd])
            near_y = out if near_y is None else jnp.concatenate([near_y, out], axis=0)
            while (sent + 1) * width <= b * pd:
                start_far(e + 1, sent, slot_pick, part(far_y, sent), 1)
                sent += 1
        return far, pick(near_y, near_out)

    base = arrive(0, own, True)
    publish(0, base)
    far_base, own = operate(1, pick(base, near_in))
    publish(3, far_base)
    forward(0)
    first = arrive(2, own, True)
    publish(1, first)
    near = pick(first, near_in)
    forward(3)
    collect(0)
    far_first, own = operate(3, near)
    forward(1)
    publish(4, far_first)
    collect(1)
    pair = rows_all[0:2 * allcase, :]
    square = exact(pair, pair, NT)
    start_gram(0, jnp.concatenate([square[0:allcase, 0:allcase], square[0:allcase, allcase:], square[allcase:, allcase:]], axis=0))
    second = arrive(4, own, False)
    publish(2, second)
    forward(4)
    collect(3)

    n = allcase
    grams = finish_gram(0)
    g00 = sym(grams[0:n])
    g01 = sym(grams[n:2 * n])
    g11 = sym(grams[2 * n:3 * n])
    step1 = gauss_solve(g01, g00)
    forward(2)
    cross = exact(g01, step1)
    g1 = sym(g00 - cross - cross.T + exact(step1, exact(g11, step1), TN))
    turn = gauss_solve(g00, g1)
    eye = jnp.where(
        lax.broadcasted_iota(jnp.int32, (n, n), 0) == lax.broadcasted_iota(jnp.int32, (n, n), 1),
        1.0,
        0.0,
    )
    lead = turn + eye
    mixed = exact(lead, exact(g11, step1), TN)
    known = exact(lead, exact(g01, lead), TN) - mixed - mixed.T

    collect(4)
    collect(2)
    start_gram(1, exact(rows_all[n:2 * n, :], rows_all[2 * n:3 * n, :], NT))
    g12 = sym(finish_gram(1))
    curve = sym(known + exact(step1, exact(g12, step1), TN))
    step2 = gauss_solve(curve, g1)
    alpha = step1 + exact(lead, step2)
    beta = exact(step1, step2)
    at = alpha.T[0:ncase]
    bt = beta.T[0:ncase]
    zero = jnp.zeros_like(at)
    coefs = jnp.concatenate(
        [
            jnp.concatenate([at, -bt, zero], axis=1),
            jnp.concatenate([zero, -at, bt], axis=1),
        ],
        axis=0,
    )
    ctop, clow = split(coefs)
    both = jnp.concatenate([ctop, clow], axis=0)
    vtop, vlow = split(rows_all[0:3 * allcase, :])
    part_a = mm(both, vtop)
    mixed_rows = part_a[0:2 * ncase] + part_a[2 * ncase:] + mm(ctop, vlow)
    for d in range(pd):
        cols = slice(d * nport, (d + 1) * nport)
        sol_ref[d] = mixed_rows[0:ncase, cols]
        res_ref[d] = nat[0, d] + mixed_rows[ncase:, cols]

    answer = jnp.concatenate([sol_ref[:, k, :] for k in range(ncase)], axis=0)
    ftop, flow = split(rows_all[3 * allcase:, :])
    lead_a = jnp.concatenate([ctop[0:ncase, 0:2 * n], clow[0:ncase, 0:2 * n]], axis=0)
    part_f = mm(lead_a, ftop)
    far_rows = part_f[0:ncase] + part_f[ncase:] + mm(ctop[0:ncase, 0:2 * n], flow)
    for d in range(pd):
        nat_far[d] = far_rows[:, d * nport:(d + 1) * nport]
    near = wide(pick(answer, near_in), pd)
    ends = jnp.concatenate(
        [near, jnp.concatenate([nat_far[:, k, :] for k in range(ncase)], axis=1)], axis=0
    )
    scaled = inv_keep[...] / stiff
    back = scaled - apply_tables(red_tab, ends)
    for k in range(ncase):
        bub_ref[:, k, :] = back[:, k * ncomp:(k + 1) * ncomp]

    wait_on(ask_send.at[rest], part_ssem.at[0])
    for e in range(5):
        for j in range(chunks):
            wait_on(far_send.at[e, j, rest], part_ssem.at[3 + e * chunks + j])
    for s in range(2):
        wait_on(gram_refs[s][1].at[rest], part_ssem.at[1 + s])
    for f in range(5):
        for i in range(1, nq):
            wait_on(nat.at[f], case_ssem.at[f, i])


def local(
    comp_type,
    stiffness,
    near_port,
    far_owner,
    far_port,
    bubble_load,
    port_load,
    bubble_inverse,
    coupling,
    port_block,
):
    npy = lax.axis_size("py")
    parts = lax.axis_size("px") * npy
    nq = lax.axis_size("case")
    ncomp = comp_type.shape[0]
    modes, ncase, _ = bubble_load.shape
    pd, _, nport = port_load.shape
    cap = 3 * ncomp // (2 * parts)
    depth = -(-cap // 8) * 8
    allcase = nq * ncase
    width = 128 if (ncase * pd) % 128 == 0 else ncase * pd
    chunks = ncase * pd // width
    idx = jnp.stack([comp_type, near_port, far_owner[:, 0], far_port])
    vmem = pl.BlockSpec(memory_space=pltpu.VMEM)

    def body(*refs):
        kernel((parts, npy, nq, depth, width, chunks), *refs)

    return pl.pallas_call(
        body,
        out_shape=(
            jax.ShapeDtypeStruct(port_load.shape, F32),
            jax.ShapeDtypeStruct(port_load.shape, F32),
            jax.ShapeDtypeStruct(bubble_load.shape, F32),
        ),
        in_specs=[vmem] * 7,
        out_specs=(vmem, vmem, vmem),
        scratch_shapes=[
            pltpu.VMEM((parts, depth, nport), F32),
            pltpu.VMEM((parts, depth, nport), F32),
            pltpu.VMEM((5, chunks, parts, depth, width), F32),
            pltpu.VMEM((5, chunks, parts, depth, width), F32),
            pltpu.VMEM((5, pd, ncase, nport), F32),
            pltpu.VMEM((5, nq, pd, ncase, nport), F32),
            pltpu.VMEM((5 * allcase, pd * nport), F32),
            pltpu.VMEM((8, 3 * allcase * allcase // 8), F32),
            pltpu.VMEM((parts, 8, 3 * allcase * allcase // 8), F32),
            pltpu.VMEM((8, allcase * allcase // 8), F32),
            pltpu.VMEM((parts, 8, allcase * allcase // 8), F32),
            pltpu.VMEM((modes, ncase * ncomp), F32),
            pltpu.VMEM((pd, ncase, nport), F32),
            pltpu.SemaphoreType.DMA((3 + 5 * chunks,)),
            pltpu.SemaphoreType.DMA((3 + 5 * chunks,)),
            pltpu.SemaphoreType.DMA((5, nq)),
            pltpu.SemaphoreType.DMA((5, nq)),
        ],
        compiler_params=pltpu.CompilerParams(
            collective_id=0, has_side_effects=True, vmem_limit_bytes=60 * 1024 * 1024
        ),
        name="condensed_solve",
    )(
        idx,
        stiffness.reshape(1, ncomp),
        bubble_load,
        port_load,
        bubble_inverse,
        jnp.swapaxes(coupling, 1, 2),
        port_block,
    )


def solution(mesh):
    placed = (
        P(("px", "py")),
        P(("px", "py")),
        P(("px", "py")),
        P(("px", "py"), None),
        P(("px", "py")),
        P(None, "case", ("px", "py")),
        P(None, "case", ("px", "py")),
        P(),
        P(),
        P(),
    )
    return jax.shard_map(
        local,
        mesh=mesh,
        in_specs=placed,
        out_specs=(
            P(None, "case", ("px", "py")),
            P(None, "case", ("px", "py")),
            P(None, "case", ("px", "py")),
        ),
        check_vma=False,
    )
```

profile of v0, /device:TPU:0, one launch (start us, length us, event | category | flops | bytes accessed | tf_op | source)
XLA Modules:
  0.0 75.6 jit_solution(17311632650527787299)
XLA Ops:
  0.6 0.0 copy-start.5
  0.6 0.0 copy-start.2
  0.7 0.0 copy-start.3
  0.7 0.0 copy-start.4
  0.7 0.6 copy-done.5
  1.3 0.0 copy-done.2
  1.3 0.0 copy-done.3
  1.3 0.0 copy-done.4
  1.3 0.6 pad_add_fusion.refs_0_
  1.9 70.3 %condensed_solve.1 = (f32[48,8,128]{2,1,0:T(8,128)}, f32[48,8,128]{2,1,0:T(8,128)}, f32[64,8,128]{2,1,0:T(8,128)}) custom-call(s32[4,128]{1,0:T(4,128)} %pad_add_fusion.refs_0_, f32[1,128]{1,0:T(1,128)} %bitcast.7, f32[64,8,128]{2,1,0:T(8,128)} %refs_2_.1, f32[48,8,128]{2,1,0:T(8,128)} %refs_3_.1, f32[8,64,64]{2,1,0:T(8,128)} %refs_4_.1, ...), custom_call_target="tpu_custom_call" | custom-call | tf_op jit(solution)/shard_map/condensed_solve/pallas_call | solution.py:435
  72.2 0.0 copy-start.1
  72.2 1.7 %copy.16 = f32[48,8,128]{2,1,0:T(8,128)} copy(f32[48,8,128]{2,1,0:T(8,128)} %get-tuple-element.6) | data formatting | bytes 393216
  73.9 0.0 copy-done.1
  73.9 0.0 copy-start
  73.9 0.7 copy.17
  74.5 0.3 copy-done
  74.9 0.7 copy.18
Async XLA Ops:
  0.6 0.7 copy-start.5
  0.6 0.7 copy-start.2
  0.7 0.7 copy-start.3
  0.7 0.7 copy-start.4
  72.2 1.7 %copy-start.1 = (f32[48,8,128]{2,1,0:T(8,128)S(1)}, f32[48,8,128]{2,1,0:T(8,128)}, u32[]{:S(2)}) copy-start(f32[48,8,128]{2,1,0:T(8,128)} %get-tuple-element.7) | copy-start | bytes 589828
  73.9 1.0 %copy-start = (f32[64,8,128]{2,1,0:T(8,128)S(1)}, f32[64,8,128]{2,1,0:T(8,128)}, u32[]{:S(2)}) copy-start(f32[64,8,128]{2,1,0:T(8,128)} %get-tuple-element.8) | copy-start | bytes 786436
where the time goes:
time: 75.8 us; the launch traced here: 75.6 us
  Pallas kernels  70.3 us (93%)
  local copies, waits for them, and re-layouts  4.05 us (5%)
    pallas_call x1, Pallas kernels, local(): pl.pallas_call(body, out_shape=(jax.ShapeDtypeStruct(port_load.shape, F32...  70.3 us
    unnamed x15, local copies, waits for them, and re-layouts  4.05 us

commit v1 on v0

v1 whole, which is shorter than its diff:
```python
import jax
import jax.numpy as jnp
from jax import lax
from jax.experimental import pallas as pl
from jax.experimental.pallas import tpu as pltpu
from jax.sharding import PartitionSpec as P

HIGH = lax.Precision.HIGHEST
F32 = jnp.float32
BF16 = jnp.bfloat16
MESH = pl.DeviceIdType.MESH
NT = (((1,), (1,)), ((), ()))
TN = (((0,), (0,)), ((), ()))


def split(x):
    top = x.astype(BF16)
    return top, (x - top.astype(F32)).astype(BF16)


def mm(a, b):
    return jnp.dot(a, b, preferred_element_type=F32)


def exact(a, b, dims=(((1,), (0,)), ((), ()))):
    return lax.dot_general(a, b, dims, precision=HIGH, preferred_element_type=F32)


def gauss_solve(matrix, target):
    n = matrix.shape[0]
    aug = jnp.concatenate([matrix, target], axis=1)
    rows = lax.broadcasted_iota(jnp.int32, aug.shape, 0)
    for j in range(0, n, 2):
        row0, row1 = aug[j:j + 1, :], aug[j + 1:j + 2, :]
        col0 = jnp.broadcast_to(aug[:, j:j + 1], aug.shape)
        col1 = jnp.broadcast_to(aug[:, j + 1:j + 2], aug.shape)
        a, c = col0[j:j + 1, :], col0[j + 1:j + 2, :]
        b, d = col1[j:j + 1, :], col1[j + 1:j + 2, :]
        scale = 1.0 / (a * d - b * c)
        new0 = (d * row0 - b * row1) * scale
        new1 = (a * row1 - c * row0) * scale
        rest = aug - col0 * new0 - col1 * new1
        aug = jnp.where(rows == j, new0, jnp.where(rows == j + 1, new1, rest))
    return aug[:, n:]


def kernel(
    sizes,
    kind_hbm,
    near_hbm,
    owner_hbm,
    far_hbm,
    stiff_hbm,
    bload_hbm,
    pload_hbm,
    binv_hbm,
    coup_hbm,
    pblock_hbm,
    sol_ref,
    res_ref,
    bub_ref,
    kind_ref,
    near_ref,
    owner_ref,
    far_ref,
    stiff_ref,
    bload_ref,
    pload_ref,
    binv_ref,
    coup_ref,
    pblock_ref,
    ask_send,
    ask_recv,
    far_send,
    far_recv,
    gath,
    image,
    rows_all,
    pair_send,
    pair_recv,
    curve_send,
    curve_recv,
    curve_mine,
    curve_all,
    inv_keep,
    nat_far,
    in_sem,
    part_ssem,
    part_rsem,
    case_ssem,
    case_rsem,
):
    parts, npy, nq, depth, width, chunks = sizes
    my_x, my_y, my_c = lax.axis_index("px"), lax.axis_index("py"), lax.axis_index("case")
    me = my_x * npy + my_y

    def part_id(step):
        other = lax.rem(me + step + parts, parts)
        return (other // npy, lax.rem(other, npy), my_c)

    def case_to(step):
        if nq == 4:
            other = my_c + (step % 2) * (1 - 2 * lax.rem(my_c, 2))
            return other + (step // 2) * (2 - 4 * (my_c // 2))
        return lax.rem(my_c + step, nq)

    def case_from(step):
        return case_to(step) if nq == 4 else lax.rem(my_c + nq - step, nq)

    def case_id(step):
        return (my_x, my_y, case_to(step))

    direct = (1, 2) if nq == 4 else tuple(range(1, nq))

    barrier = pltpu.get_barrier_semaphore()

    def greet_part(i, _):
        pl.semaphore_signal(barrier, inc=1, device_id=part_id(i), device_id_type=MESH)
        return 0

    lax.fori_loop(1, parts, greet_part, 0)
    for i in range(1, nq):
        pl.semaphore_signal(barrier, inc=1, device_id=case_id(i), device_id_type=MESH)

    inputs = (
        (near_hbm, near_ref),
        (owner_hbm, owner_ref),
        (far_hbm, far_ref),
        (kind_hbm, kind_ref),
        (binv_hbm, binv_ref),
        (bload_hbm, bload_ref),
        (coup_hbm, coup_ref),
        (stiff_hbm, stiff_ref),
        (pload_hbm, pload_ref),
        (pblock_hbm, pblock_ref),
    )
    fetches = [
        pltpu.make_async_copy(src, dst, in_sem.at[i]) for i, (src, dst) in enumerate(inputs)
    ]
    for fetch in fetches:
        fetch.start()

    kinds = binv_ref.shape[0]
    modes, ncase, ncomp = bload_ref.shape
    pd = pload_ref.shape[0]
    nport = pload_ref.shape[2]
    slots = parts * depth
    allcase = nq * ncase

    for fetch in fetches[0:4]:
        fetch.wait()
    kind_row = kind_ref[...]
    near_row = near_ref[...]
    owner_row = owner_ref[...]
    far_row = far_ref[...]

    def as_column(row):
        return jnp.broadcast_to(row.astype(F32), (ncomp, ncomp)).T

    sub = lax.broadcasted_iota(jnp.int32, (ncomp, ncomp), 0)
    lane = lax.broadcasted_iota(jnp.int32, (ncomp, ncomp), 1)
    same = (as_column(owner_row) == owner_row.astype(F32)) & (sub < lane)
    rank = jnp.sum(jnp.where(same, 1.0, 0.0), axis=0, keepdims=True).astype(jnp.int32)
    step_row = lax.rem(owner_row - me + parts, parts)
    slot_row = step_row * depth + rank
    slot_sub = lax.broadcasted_iota(jnp.int32, (slots, ncomp), 0)
    slot_pick = jnp.where(slot_sub == slot_row, 1.0, 0.0).astype(BF16)
    step_sub = lax.broadcasted_iota(jnp.int32, (parts, ncomp), 0)
    naming = jnp.where(step_sub == step_row, (far_row + 1).astype(F32), 0.0)
    ranked = jnp.where(sub == rank, 1.0, 0.0)
    wanted = exact(naming, ranked, NT) - 1.0
    wanted = wanted.reshape(parts, 1, ncomp)
    ask_send[...] = wanted
    ask_recv[0] = wanted[0]
    near_in = jnp.where(sub == near_row, 1.0, 0.0).astype(BF16)
    near_out = jnp.where(lane.astype(F32) == as_column(near_row), 1.0, 0.0).astype(BF16)

    order = sorted(range(1, parts), key=lambda i: -min(i % npy, npy - i % npy))

    def send_parts(src, dst, e, sign):
        def body(i, _):
            pltpu.make_async_remote_copy(
                src_ref=src(i),
                dst_ref=dst(i),
                send_sem=part_ssem.at[e],
                recv_sem=part_rsem.at[e],
                device_id=part_id(i if sign > 0 else -i),
                device_id_type=MESH,
            ).start()
            return 0

        if parts <= 8:
            for i in order:
                body(i, 0)
        else:
            lax.fori_loop(1, parts, body, 0)

    def wait_on(ref, sem):
        pltpu.make_async_copy(ref, ref, sem).wait()

    rest = pl.ds(1, parts - 1)

    def tile_cases(row):
        return jnp.concatenate([row] * ncase, axis=1)

    kind_all = tile_cases(kind_row)
    masks = [jnp.where(kind_all == t, 1.0, 0.0).astype(BF16) for t in range(kinds)]

    def apply_tables(tab, x):
        top, low = split(x)
        lanes = x.shape[1]
        xt = jnp.concatenate([top * m[:, :lanes] for m in masks], axis=0)
        xl = jnp.concatenate([low * m[:, :lanes] for m in masks], axis=0)
        return mm(tab[0], xt) + mm(tab[0], xl) + mm(tab[1], xt)

    def wide(field, rows):
        return jnp.concatenate(
            [field[k * rows:(k + 1) * rows] for k in range(field.shape[0] // rows)], axis=1
        )

    def tall(x):
        return jnp.concatenate(
            [x[:, k * ncomp:(k + 1) * ncomp] for k in range(x.shape[1] // ncomp)], axis=0
        )

    def pick(x, onehot):
        top, low = split(x)
        return mm(jnp.concatenate([top, low], axis=1), jnp.concatenate([onehot, onehot], axis=0))

    def start_far(e, j, onehot, x, sign):
        top, low = split(x)
        out = lax.dot_general(
            jnp.concatenate([onehot, onehot], axis=1),
            jnp.concatenate([top, low], axis=1),
            NT,
            preferred_element_type=F32,
        ).reshape(parts, depth, width)
        far_send[e, j] = out
        far_recv[e, j, 0] = out[0]
        send_parts(
            lambda i: far_send.at[e, j, i], lambda i: far_recv.at[e, j, i], 3 + e * chunks + j, sign
        )

    def finish_far(e, j, onehot):
        wait_on(far_recv.at[e, j, rest], part_rsem.at[3 + e * chunks + j])
        got = far_recv[e, j].reshape(slots, width).T
        top, low = split(got)
        return mm(top, onehot) + mm(low, onehot)

    def send_case(f, src, dst, sem, step):
        pltpu.make_async_remote_copy(
            src_ref=src,
            dst_ref=dst,
            send_sem=case_ssem.at[f, sem],
            recv_sem=case_rsem.at[f, sem],
            device_id=case_id(step),
            device_id_type=MESH,
        ).start()

    def publish(f, field):
        for k in range(ncase):
            gath[f, my_c, :, k, :] = field[k * pd:(k + 1) * pd]
        for i in reversed(direct):
            send_case(f, gath.at[f, my_c], gath.at[f, my_c], i, i)

    def forward(f):
        if nq == 4:
            block = gath.at[f, case_from(2)]
            wait_on(block, case_rsem.at[f, 2])
            send_case(f, block, block, 3, 1)

    def collect(f):
        for i in range(1, nq):
            if nq != 4 or i != 2:
                wait_on(gath.at[f, case_from(i)], case_rsem.at[f, i])

        def body(d, _):
            cols = pl.ds(pl.multiple_of(d * nport, nport), nport)
            for q in range(nq):
                rows_all[pl.ds(f * allcase + q * ncase, ncase), cols] = gath[f, q, d]
            return 0

        lax.fori_loop(0, pd, body, 0, unroll=4)

    def field_rows(f, count=1):
        return rows_all[f * allcase:(f + count) * allcase, :]

    def image_rows(s, field):
        for k in range(ncase):
            image[s, :, k, :] = field[k * pd:(k + 1) * pd]
        return jnp.concatenate([image[s, d] for d in range(pd)], axis=1)

    def start_gram(value):
        folded = jnp.concatenate(
            [value[8 * r:8 * r + 8] for r in range(value.shape[0] // 8)], axis=1
        )
        pair_send[...] = folded
        pair_recv[0] = folded
        send_parts(lambda i: pair_send, lambda i: pair_recv.at[i], 1, 1)

    def finish_gram():
        wait_on(pair_recv.at[rest], part_rsem.at[1])
        total = jnp.sum(pair_recv[...], axis=0)
        return jnp.concatenate(
            [total[:, allcase * r:allcase * (r + 1)] for r in range(total.shape[1] // allcase)],
            axis=0,
        )

    def sym(g):
        return 0.5 * (g + g.T)

    def part(x, j):
        return x[j * width:(j + 1) * width]

    for fetch in fetches[4:7]:
        fetch.wait()
    inv_tab = split(jnp.concatenate([binv_ref[t] for t in range(kinds)], axis=1))
    coup_tab = split(jnp.concatenate([coup_ref[t].T for t in range(kinds)], axis=1))
    loads = jnp.concatenate([bload_ref[:, k, :] for k in range(ncase)], axis=1)
    lifted = apply_tables(inv_tab, loads)
    inv_keep[...] = lifted
    condensed = -apply_tables(coup_tab, lifted)
    leaving = tall(condensed[pd:])
    pl.semaphore_wait(barrier, parts - 1 + nq - 1)
    send_parts(lambda i: ask_send.at[i], lambda i: ask_recv.at[i], 0, 1)
    for j in range(chunks):
        start_far(0, j, slot_pick, part(leaving, j), 1)
    for fetch in fetches[7:]:
        fetch.wait()
    stiff = tile_cases(stiff_ref[...])
    red_t = [exact(binv_ref[t], coup_ref[t], TN) for t in range(kinds)]
    schur = [pblock_ref[t] - exact(red_t[t], coup_ref[t], TN) for t in range(kinds)]
    schur_tab = split(jnp.concatenate(schur, axis=1))
    red_tab = split(jnp.concatenate(red_t, axis=1))
    own = jnp.concatenate([pload_ref[:, k, :] for k in range(ncase)], axis=0)
    own = own + pick(tall(condensed[:pd]), near_out)
    wait_on(ask_recv.at[rest], part_rsem.at[0])
    asked = ask_recv[...].reshape(parts, ncomp)
    asked = jnp.concatenate([asked] * (ncomp // parts), axis=0).T
    port_lane = lax.broadcasted_iota(jnp.int32, (depth, nport), 1).astype(F32)
    asked_pick = jnp.concatenate(
        [jnp.where(asked[0:depth, i:i + 1] == port_lane, 1.0, 0.0) for i in range(parts)], axis=0
    ).astype(BF16)

    def arrive(e, own, onward):
        pieces = []
        for j in range(chunks):
            piece = part(own, j) + finish_far(e, j, asked_pick)
            if onward:
                start_far(e + 1, j, asked_pick, piece, -1)
            pieces.append(piece)
        return jnp.concatenate(pieces, axis=0)

    def operate(e, near, between):
        cuts = [0, ((chunks - 1) * width) // pd, ncase] if chunks > 1 else [0, ncase]
        far, near_y, far_y, sent, have = None, None, None, 0, 0
        for a, b in zip(cuts[:-1], cuts[1:]):
            if b == ncase:
                between()
            while have * width < b * pd:
                piece = finish_far(e, have, slot_pick)
                far = piece if far is None else jnp.concatenate([far, piece], axis=0)
                have += 1
            rows = slice(a * pd, b * pd)
            ends = jnp.concatenate([wide(near[rows], pd), wide(far[rows], pd)], axis=0)
            y = apply_tables(schur_tab, ends) * stiff[:, a * ncomp:b * ncomp]
            out = tall(y[pd:])
            far_y = out if far_y is None else jnp.concatenate([far_y, out], axis=0)
            out = tall(y[:pd])
            near_y = out if near_y is None else jnp.concatenate([near_y, out], axis=0)
            while (sent + 1) * width <= b * pd:
                start_far(e + 1, sent, slot_pick, part(far_y, sent), 1)
                sent += 1
        return far, far_y, pick(near_y, near_out)

    base = arrive(0, own, True)
    publish(0, base)
    far_base, _, own = operate(1, pick(base, near_in), lambda: forward(0))
    publish(3, far_base)
    first = arrive(2, own, True)
    publish(1, first)
    near = pick(first, near_in)
    forward(3)
    collect(0)
    far_first, far_image, own = operate(3, near, lambda: forward(1))
    publish(4, far_first)
    collect(1)
    pair = field_rows(0, 2)
    square = exact(pair, pair, NT)
    start_gram(
        jnp.concatenate(
            [
                square[0:allcase, 0:allcase],
                square[0:allcase, allcase:],
                square[allcase:, allcase:],
            ],
            axis=0,
        )
    )
    near_curve = exact(image_rows(0, own), field_rows(1), NT)
    far_lines = image_rows(1, far_image)
    second = arrive(4, own, False)
    publish(2, second)
    forward(4)
    collect(4)

    n = allcase
    curve = near_curve + exact(far_lines, field_rows(4), NT)
    curve = jnp.concatenate([curve, jnp.zeros((ncase, 128 - n), F32)], axis=1)
    curve_send[...] = curve
    curve_recv[0] = curve
    send_parts(lambda i: curve_send, lambda i: curve_recv.at[i], 2, 1)

    grams = finish_gram()
    g00 = sym(grams[0:n])
    g01 = sym(grams[n:2 * n])
    g11 = sym(grams[2 * n:3 * n])
    both = gauss_solve(g01, jnp.concatenate([g00, g11], axis=1))
    forward(2)
    image_both = exact(g11, both)
    mine = jnp.where(
        lax.broadcasted_iota(jnp.int32, (n, ncase), 0)
        == lax.broadcasted_iota(jnp.int32, (n, ncase), 1) + my_c * ncase,
        1.0,
        0.0,
    )
    chosen = exact(jnp.concatenate([image_both[:, 0:n] - g01, both[:, 0:n]], axis=0), mine)

    wait_on(curve_recv.at[rest], part_rsem.at[2])
    total = jnp.sum(curve_recv[...], axis=0)
    curve_mine[...] = total
    curve_all[my_c] = total
    for i in range(1, nq):
        send_case(5, curve_mine, curve_all.at[my_c], i, i)
    collect(3)
    for i in range(1, nq):
        wait_on(curve_all.at[case_from(i)], case_rsem.at[5, i])
    g12 = curve_all[...].reshape(n, 128)[:, 0:n]
    beta = gauss_solve(sym(g12) - sym(image_both[:, n:2 * n]), chosen[0:n])
    alpha = chosen[n:2 * n] + exact(both[:, n:2 * n], beta)
    coefs = jnp.concatenate([alpha, -beta], axis=0).T
    ctop, clow = split(coefs)
    stack = jnp.concatenate([ctop, clow], axis=0)

    def mix(f):
        vtop, vlow = split(field_rows(f, 2))
        lead = mm(stack, vtop)
        return lead[0:ncase] + lead[ncase:] + mm(ctop, vlow)

    answer_rows = mix(0)
    for d in range(pd):
        sol_ref[d] = answer_rows[:, d * nport:(d + 1) * nport]
    far_rows = mix(3)
    for d in range(pd):
        nat_far[d] = far_rows[:, d * nport:(d + 1) * nport]
    answer = jnp.concatenate([sol_ref[:, k, :] for k in range(ncase)], axis=0)
    near = wide(pick(answer, near_in), pd)
    ends = jnp.concatenate(
        [near, jnp.concatenate([nat_far[:, k, :] for k in range(ncase)], axis=1)], axis=0
    )
    scaled = inv_keep[...] / stiff
    back = scaled - apply_tables(red_tab, ends)
    for k in range(ncase):
        bub_ref[:, k, :] = back[:, k * ncomp:(k + 1) * ncomp]
    collect(2)
    drop_rows = mix(1)
    for d in range(pd):
        res_ref[d] = gath[0, my_c, d] - drop_rows[:, d * nport:(d + 1) * nport]

    wait_on(ask_send.at[rest], part_ssem.at[0])
    for e in range(5):
        for j in range(chunks):
            wait_on(far_send.at[e, j, rest], part_ssem.at[3 + e * chunks + j])
    wait_on(pair_recv.at[rest], part_ssem.at[1])
    wait_on(curve_recv.at[rest], part_ssem.at[2])
    for f in range(5):
        for i in range(1, nq):
            wait_on(gath.at[f, my_c], case_ssem.at[f, i])
    for i in range(1, nq):
        wait_on(curve_mine, case_ssem.at[5, i])


def emit(*refs):
    count = len(refs) // 2
    sems = refs[-1]
    copies = [
        pltpu.make_async_copy(refs[i], refs[count + i], sems.at[i]) for i in range(count)
    ]
    for copy in copies:
        copy.start()
    for copy in copies:
        copy.wait()


def local(
    comp_type,
    stiffness,
    near_port,
    far_owner,
    far_port,
    bubble_load,
    port_load,
    bubble_inverse,
    coupling,
    port_block,
):
    npy = lax.axis_size("py")
    parts = lax.axis_size("px") * npy
    nq = lax.axis_size("case")
    ncomp = comp_type.shape[0]
    modes, ncase, _ = bubble_load.shape
    pd, _, nport = port_load.shape
    kinds = bubble_inverse.shape[0]
    cap = 3 * ncomp // (2 * parts)
    depth = -(-cap // 8) * 8
    allcase = nq * ncase
    width = 128 if (ncase * pd) % 128 == 0 else ncase * pd
    chunks = ncase * pd // width
    vmem = pl.BlockSpec(memory_space=pltpu.VMEM)
    hbm = pl.BlockSpec(memory_space=pltpu.HBM)

    def body(*refs):
        kernel((parts, npy, nq, depth, width, chunks), *refs)

    shapes = (
        jax.ShapeDtypeStruct(port_load.shape, F32),
        jax.ShapeDtypeStruct(port_load.shape, F32),
        jax.ShapeDtypeStruct(bubble_load.shape, F32),
    )
    results = pl.pallas_call(
        body,
        out_shape=shapes,
        in_specs=[hbm] * 10,
        out_specs=(vmem, vmem, vmem),
        scratch_shapes=[
            pltpu.VMEM((1, ncomp), jnp.int32),
            pltpu.VMEM((1, ncomp), jnp.int32),
            pltpu.VMEM((1, ncomp), jnp.int32),
            pltpu.VMEM((1, ncomp), jnp.int32),
            pltpu.VMEM((1, ncomp), F32),
            pltpu.VMEM(bubble_load.shape, F32),
            pltpu.VMEM(port_load.shape, F32),
            pltpu.VMEM(bubble_inverse.shape, F32),
            pltpu.VMEM((kinds, modes, 2 * pd), F32),
            pltpu.VMEM(port_block.shape, F32),
            pltpu.VMEM((parts, 1, ncomp), F32),
            pltpu.VMEM((parts, 1, ncomp), F32),
            pltpu.VMEM((5, chunks, parts, depth, width), F32),
            pltpu.VMEM((5, chunks, parts, depth, width), F32),
            pltpu.VMEM((5, nq, pd, ncase, nport), F32),
            pltpu.VMEM((2, pd, ncase, nport), F32),
            pltpu.VMEM((5 * allcase, pd * nport), F32),
            pltpu.VMEM((8, 3 * allcase * allcase // 8), F32),
            pltpu.VMEM((parts, 8, 3 * allcase * allcase // 8), F32),
            pltpu.VMEM((ncase, 128), F32),
            pltpu.VMEM((parts, ncase, 128), F32),
            pltpu.VMEM((ncase, 128), F32),
            pltpu.VMEM((nq, ncase, 128), F32),
            pltpu.VMEM((modes, ncase * ncomp), F32),
            pltpu.VMEM((pd, ncase, nport), F32),
            pltpu.SemaphoreType.DMA((10,)),
            pltpu.SemaphoreType.DMA((3 + 5 * chunks,)),
            pltpu.SemaphoreType.DMA((3 + 5 * chunks,)),
            pltpu.SemaphoreType.DMA((6, nq)),
            pltpu.SemaphoreType.DMA((6, nq)),
        ],
        compiler_params=pltpu.CompilerParams(
            collective_id=0, has_side_effects=True, vmem_limit_bytes=32 * 1024 * 1024
        ),
        name="condensed_solve",
    )(
        comp_type.reshape(1, ncomp),
        near_port.reshape(1, ncomp),
        far_owner.reshape(1, ncomp),
        far_port.reshape(1, ncomp),
        stiffness.reshape(1, ncomp),
        bubble_load,
        port_load,
        bubble_inverse,
        jnp.swapaxes(coupling, 1, 2),
        port_block,
    )
    return pl.pallas_call(
        emit,
        out_shape=shapes,
        in_specs=[vmem] * 3,
        out_specs=(hbm, hbm, hbm),
        scratch_shapes=[pltpu.SemaphoreType.DMA((3,))],
        compiler_params=pltpu.CompilerParams(vmem_limit_bytes=4 * 1024 * 1024),
        name="emit",
    )(*results)


def solution(mesh):
    placed = (
        P(("px", "py")),
        P(("px", "py")),
        P(("px", "py")),
        P(("px", "py"), None),
        P(("px", "py")),
        P(None, "case", ("px", "py")),
        P(None, "case", ("px", "py")),
        P(),
        P(),
        P(),
    )
    return jax.shard_map(
        local,
        mesh=mesh,
        in_specs=placed,
        out_specs=(
            P(None, "case", ("px", "py")),
            P(None, "case", ("px", "py")),
            P(None, "case", ("px", "py")),
        ),
        check_vma=False,
    )
```

time: 75.8 us -> 67.7 us (0.89)
  Pallas kernels: 70.3 us -> 61.1 us
  local copies, waits for them, and re-layouts: 4.05 us -> 5.45 us
    pallas_call x1 -> x2, Pallas kernels: 70.3 us -> 61.1 us  [the longest x1 60.2 us: local(): pl.pallas_call(body, out_shape=shapes, in_specs=[hbm] * 10, out_specs=(vm...]
    unnamed x15 -> x20, local copies, waits for them, and re-layouts: 4.05 us -> 5.45 us
where the time goes in v1:
time: 67.7 us; the launch traced here: 67.4 us
  Pallas kernels  61.1 us (90%)
  local copies, waits for them, and re-layouts  5.45 us (8%)
  between operations  0.85 us (1%)
    pallas_call x1, Pallas kernels, local(): pl.pallas_call(body, out_shape=shapes, in_specs=[hbm] * 10, out_specs=(vm...  60.2 us
    unnamed x20, local copies, waits for them, and re-layouts  5.45 us

profile of v1, /device:TPU:0, one launch (start us, length us, event | category | flops | bytes accessed | tf_op | source)
XLA Modules:
  0.0 67.4 jit_solution(13738984525255449801)
XLA Ops:
  0.6 0.0 copy-start.8
  0.6 0.0 copy-start.9
  0.7 0.0 copy-start.5
  0.7 0.0 copy-start.6
  0.7 0.0 copy-start.7
  0.7 0.6 copy-done.8
  1.3 0.0 copy-done.9
  1.3 0.0 copy-done.5
  1.3 0.0 copy-done.6
  1.3 0.0 copy-done.7
  1.4 0.0 copy-start
  1.4 1.0 %copy-done = f32[8,96,96]{2,1,0:T(8,128)S(1)} copy-done((f32[8,96,96]{2,1,0:T(8,128)S(1)}, f32[8,96,96]{2,1,0:T(8,128)}, u32[]{:S(2)}) %copy-start) | copy-done | bytes 294936
  2.4 0.0 copy-start.1
  2.4 0.9 %copy-done.1 = f32[64,8,128]{2,1,0:T(8,128)S(1)} copy-done((f32[64,8,128]{2,1,0:T(8,128)S(1)}, f32[64,8,128]{2,1,0:T(8,128)}, u32[]{:S(2)}) %copy-start.1) | copy-done | bytes 262168
  3.3 0.0 copy-start.2
  3.3 0.9 %copy-done.2 = f32[8,64,64]{2,1,0:T(8,128)S(1)} copy-done((f32[8,64,64]{2,1,0:T(8,128)S(1)}, f32[8,64,64]{2,1,0:T(8,128)}, u32[]{:S(2)}) %copy-start.2) | copy-done | bytes 131096
  4.3 0.0 copy-start.3
  4.3 0.9 %copy-done.3 = f32[8,96,64]{1,2,0:T(8,128)S(1)} copy-done((f32[8,96,64]{1,2,0:T(8,128)S(1)}, f32[8,96,64]{1,2,0:T(8,128)}, u32[]{:S(2)}) %copy-start.3) | copy-done | bytes 196632
  5.2 0.0 copy-start.4
  5.2 0.9 %copy-done.4 = f32[48,8,128]{2,1,0:T(8,128)S(1)} copy-done((f32[48,8,128]{2,1,0:T(8,128)S(1)}, f32[48,8,128]{2,1,0:T(8,128)}, u32[]{:S(2)}) %copy-start.4) | copy-done | bytes 196632
  6.1 60.2 %condensed_solve.1 = (f32[48,8,128]{2,1,0:T(8,128)S(1)}, f32[48,8,128]{2,1,0:T(8,128)S(1)}, f32[64,8,128]{2,1,0:T(8,128)S(1)}) custom-call(s32[1,128]{1,0:T(1,128)S(1)} %bitcast.7, s32[1,128]{1,0:T(1,128)S(1)} %bitcast.8, s32[1,128]{1,0:T(1,128)S(1)} %bitcast.9, s32[1,128]{1,0:T(1,128)S(1)} %bitcast.10, f32[1,128]{1,0:T(1,128)S(1)} %bitcast.11, ...), custom_call_target="tpu_custom_call" | custom-call | tf_op jit(solution)/shard_map/condensed_solve/pallas_call | solution.py:530
  66.4 0.9 %emit.1 = (f32[48,8,128]{2,1,0:T(8,128)}, f32[48,8,128]{2,1,0:T(8,128)}, f32[64,8,128]{2,1,0:T(8,128)}) custom-call(f32[48,8,128]{2,1,0:T(8,128)S(1)} %get-tuple-element.6.refs_0_, f32[48,8,128]{2,1,0:T(8,128)S(1)} %get-tuple-element.7.refs_1_, f32[64,8,128]{2,1,0:T(8,128)S(1)} %get-tuple-element.8.refs_2_), custom_call_target="tpu_custom_call" | custom-call | tf_op jit(solution)/shard_map/emit/pallas_call | solution.py:583
Async XLA Ops:
  0.6 0.7 copy-start.8
  0.6 0.7 copy-start.9
  0.7 0.7 copy-start.5
  0.7 0.7 copy-start.6
  0.7 0.7 %copy-start.7 = (s32[128,1]{0,1:T(1,128)S(1)}, s32[128,1]{0,1:T(1,128)}, u32[]{:S(2)}) copy-start(s32[128,1]{0,1:T(1,128)} %param.13) | copy-start | bytes 1540
  1.4 1.0 %copy-start = (f32[8,96,96]{2,1,0:T(8,128)S(1)}, f32[8,96,96]{2,1,0:T(8,128)}, u32[]{:S(2)}) copy-start(f32[8,96,96]{2,1,0:T(8,128)} %refs_9_.1) | copy-start | bytes 884740
  2.4 0.9 %copy-start.1 = (f32[64,8,128]{2,1,0:T(8,128)S(1)}, f32[64,8,128]{2,1,0:T(8,128)}, u32[]{:S(2)}) copy-start(f32[64,8,128]{2,1,0:T(8,128)} %refs_5_.1) | copy-start | bytes 786436
  3.3 0.9 %copy-start.2 = (f32[8,64,64]{2,1,0:T(8,128)S(1)}, f32[8,64,64]{2,1,0:T(8,128)}, u32[]{:S(2)}) copy-start(f32[8,64,64]{2,1,0:T(8,128)} %refs_7_.1) | copy-start | bytes 393220
  4.3 0.9 %copy-start.3 = (f32[8,96,64]{1,2,0:T(8,128)S(1)}, f32[8,96,64]{1,2,0:T(8,128)}, u32[]{:S(2)}) copy-start(f32[8,96,64]{1,2,0:T(8,128)} %param.18) | copy-start | bytes 589828
  5.2 0.9 %copy-start.4 = (f32[48,8,128]{2,1,0:T(8,128)S(1)}, f32[48,8,128]{2,1,0:T(8,128)}, u32[]{:S(2)}) copy-start(f32[48,8,128]{2,1,0:T(8,128)} %refs_6_.1) | copy-start | bytes 589828

commit v2 on v1

--- a/solution.py
+++ b/solution.py
@@ -569,16 +569,21 @@
         ),
         name="condensed_solve",
     )(
-        comp_type.reshape(1, ncomp),
-        near_port.reshape(1, ncomp),
-        far_owner.reshape(1, ncomp),
-        far_port.reshape(1, ncomp),
-        stiffness.reshape(1, ncomp),
-        bubble_load,
-        port_load,
-        bubble_inverse,
-        jnp.swapaxes(coupling, 1, 2),
-        port_block,
+        *(
+            pltpu.with_memory_space_constraint(x, pltpu.HBM)
+            for x in (
+                comp_type.reshape(1, ncomp),
+                near_port.reshape(1, ncomp),
+                far_owner.reshape(1, ncomp),
+                far_port.reshape(1, ncomp),
+                stiffness.reshape(1, ncomp),
+                bubble_load,
+                port_load,
+                bubble_inverse,
+                jnp.swapaxes(coupling, 1, 2),
+                port_block,
+            )
+        )
     )
     return pl.pallas_call(
         emit,

time: 67.7 us -> 62.2 us (0.919)
  local copies, waits for them, and re-layouts: 5.45 us -> 0 us
    unnamed x20 -> x0, local copies, waits for them, and re-layouts: 5.45 us -> none
where the time goes in v2:
time: 62.2 us; the launch traced here: 62 us
  Pallas kernels  61.2 us (98%)
  between operations  0.8 us (1%)
    pallas_call x1, Pallas kernels, local(): pl.pallas_call(body, out_shape=shapes, in_specs=[hbm] * 10, out_specs=(vm...  60.4 us

profile of v2, /device:TPU:0, one launch (start us, length us, event | category | flops | bytes accessed | tf_op | source)
XLA Modules:
  0.0 62.0 jit_solution(14987380447762312996)
XLA Ops:
  0.6 60.4 %condensed_solve.1 = (f32[48,8,128]{2,1,0:T(8,128)S(1)}, f32[48,8,128]{2,1,0:T(8,128)S(1)}, f32[64,8,128]{2,1,0:T(8,128)S(1)}) custom-call(s32[1,128]{1,0:T(1,128)} %bitcast.7, s32[1,128]{1,0:T(1,128)} %bitcast.8, s32[1,128]{1,0:T(1,128)} %bitcast.9, s32[1,128]{1,0:T(1,128)} %bitcast.10, f32[1,128]{1,0:T(1,128)} %bitcast.11, f32[64,8,128]{2,1,0:T(8,128)} %refs_5_.1, ...), custom_call_target="tpu_custom_call" | custom-call | tf_op jit(solution)/shard_map/condensed_solve/pallas_call | solution.py:530
  61.0 0.9 %emit.1 = (f32[48,8,128]{2,1,0:T(8,128)}, f32[48,8,128]{2,1,0:T(8,128)}, f32[64,8,128]{2,1,0:T(8,128)}) custom-call(f32[48,8,128]{2,1,0:T(8,128)S(1)} %get-tuple-element.6.refs_0_, f32[48,8,128]{2,1,0:T(8,128)S(1)} %get-tuple-element.7.refs_1_, f32[64,8,128]{2,1,0:T(8,128)S(1)} %get-tuple-element.8.refs_2_), custom_call_target="tpu_custom_call" | custom-call | tf_op jit(solution)/shard_map/emit/pallas_call | solution.py:588

commit v3 on v2

--- a/solution.py
+++ b/solution.py
@@ -74,7 +74,6 @@
     far_send,
     far_recv,
     gath,
-    image,
     rows_all,
     pair_send,
     pair_recv,
@@ -127,10 +126,10 @@
         (owner_hbm, owner_ref),
         (far_hbm, far_ref),
         (kind_hbm, kind_ref),
+        (stiff_hbm, stiff_ref),
         (binv_hbm, binv_ref),
         (bload_hbm, bload_ref),
         (coup_hbm, coup_ref),
-        (stiff_hbm, stiff_ref),
         (pload_hbm, pload_ref),
         (pblock_hbm, pblock_ref),
     )
@@ -147,7 +146,7 @@
     slots = parts * depth
     allcase = nq * ncase
 
-    for fetch in fetches[0:4]:
+    for fetch in fetches[0:5]:
         fetch.wait()
     kind_row = kind_ref[...]
     near_row = near_ref[...]
@@ -166,14 +165,22 @@
     slot_sub = lax.broadcasted_iota(jnp.int32, (slots, ncomp), 0)
     slot_pick = jnp.where(slot_sub == slot_row, 1.0, 0.0).astype(BF16)
     step_sub = lax.broadcasted_iota(jnp.int32, (parts, ncomp), 0)
-    naming = jnp.where(step_sub == step_row, (far_row + 1).astype(F32), 0.0)
+    naming = jnp.concatenate(
+        [
+            jnp.where(step_sub == step_row, row, 0.0)
+            for row in ((far_row + 1).astype(F32), kind_row.astype(F32), stiff_ref[...])
+        ],
+        axis=0,
+    )
     ranked = jnp.where(sub == rank, 1.0, 0.0)
-    wanted = exact(naming, ranked, NT) - 1.0
-    wanted = wanted.reshape(parts, 1, ncomp)
+    wanted = exact(naming, ranked, NT)
+    wanted = jnp.concatenate([wanted[r * parts:(r + 1) * parts] for r in range(3)], axis=1)
+    wanted = wanted.reshape(parts, 1, 3 * ncomp)
     ask_send[...] = wanted
     ask_recv[0] = wanted[0]
     near_in = jnp.where(sub == near_row, 1.0, 0.0).astype(BF16)
     near_out = jnp.where(lane.astype(F32) == as_column(near_row), 1.0, 0.0).astype(BF16)
+    near_slots = lax.dot_general(slot_pick, near_in, NT, preferred_element_type=F32).astype(BF16)
 
     order = sorted(range(1, parts), key=lambda i: -min(i % npy, npy - i % npy))
 
@@ -203,49 +210,62 @@
     def tile_cases(row):
         return jnp.concatenate([row] * ncase, axis=1)
 
-    kind_all = tile_cases(kind_row)
-    masks = [jnp.where(kind_all == t, 1.0, 0.0).astype(BF16) for t in range(kinds)]
-
-    def apply_tables(tab, x):
+    def kind_masks(row):
+        row = tile_cases(row)
+        return [jnp.where(row == t, 1.0, 0.0).astype(BF16) for t in range(kinds)]
+
+    masks = kind_masks(kind_row)
+
+    def table(parts_of):
+        top, low = split(parts_of)
+        return top, jnp.concatenate([top, low], axis=0)
+
+    def apply_tables(tab, x, masks):
         top, low = split(x)
         lanes = x.shape[1]
         xt = jnp.concatenate([top * m[:, :lanes] for m in masks], axis=0)
         xl = jnp.concatenate([low * m[:, :lanes] for m in masks], axis=0)
-        return mm(tab[0], xt) + mm(tab[0], xl) + mm(tab[1], xt)
+        lead = mm(tab[1], xt)
+        rows = tab[0].shape[0]
+        return lead[:rows] + lead[rows:] + mm(tab[0], xl)
 
     def wide(field, rows):
         return jnp.concatenate(
             [field[k * rows:(k + 1) * rows] for k in range(field.shape[0] // rows)], axis=1
         )
 
-    def tall(x):
+    def tall(x, count):
         return jnp.concatenate(
-            [x[:, k * ncomp:(k + 1) * ncomp] for k in range(x.shape[1] // ncomp)], axis=0
+            [x[:, k * count:(k + 1) * count] for k in range(x.shape[1] // count)], axis=0
         )
 
     def pick(x, onehot):
         top, low = split(x)
         return mm(jnp.concatenate([top, low], axis=1), jnp.concatenate([onehot, onehot], axis=0))
 
-    def start_far(e, j, onehot, x, sign):
+    def at_slots(onehot, x):
         top, low = split(x)
-        out = lax.dot_general(
+        return lax.dot_general(
             jnp.concatenate([onehot, onehot], axis=1),
             jnp.concatenate([top, low], axis=1),
             NT,
             preferred_element_type=F32,
-        ).reshape(parts, depth, width)
+        )
+
+    def place(x, onehot):
+        top, low = split(x)
+        return mm(top, onehot) + mm(low, onehot)
+
+    def take_far(e, j):
+        wait_on(far_recv.at[e, j, rest], part_rsem.at[3 + e * chunks + j])
+        return far_recv[e, j].reshape(slots, width).T
+
+    def post(e, j, out, sign):
         far_send[e, j] = out
         far_recv[e, j, 0] = out[0]
         send_parts(
             lambda i: far_send.at[e, j, i], lambda i: far_recv.at[e, j, i], 3 + e * chunks + j, sign
         )
-
-    def finish_far(e, j, onehot):
-        wait_on(far_recv.at[e, j, rest], part_rsem.at[3 + e * chunks + j])
-        got = far_recv[e, j].reshape(slots, width).T
-        top, low = split(got)
-        return mm(top, onehot) + mm(low, onehot)
 
     def send_case(f, src, dst, sem, step):
         pltpu.make_async_remote_copy(
@@ -285,11 +305,6 @@
     def field_rows(f, count=1):
         return rows_all[f * allcase:(f + count) * allcase, :]
 
-    def image_rows(s, field):
-        for k in range(ncase):
-            image[s, :, k, :] = field[k * pd:(k + 1) * pd]
-        return jnp.concatenate([image[s, d] for d in range(pd)], axis=1)
-
     def start_gram(value):
         folded = jnp.concatenate(
             [value[8 * r:8 * r + 8] for r in range(value.shape[0] // 8)], axis=1
@@ -312,100 +327,114 @@
     def part(x, j):
         return x[j * width:(j + 1) * width]
 
-    for fetch in fetches[4:7]:
+    for fetch in fetches[5:8]:
         fetch.wait()
-    inv_tab = split(jnp.concatenate([binv_ref[t] for t in range(kinds)], axis=1))
-    coup_tab = split(jnp.concatenate([coup_ref[t].T for t in range(kinds)], axis=1))
+    inv_tab = table(jnp.concatenate([binv_ref[t] for t in range(kinds)], axis=1))
+    coup_tab = table(jnp.concatenate([coup_ref[t].T for t in range(kinds)], axis=1))
     loads = jnp.concatenate([bload_ref[:, k, :] for k in range(ncase)], axis=1)
-    lifted = apply_tables(inv_tab, loads)
+    lifted = apply_tables(inv_tab, loads, masks)
     inv_keep[...] = lifted
-    condensed = -apply_tables(coup_tab, lifted)
-    leaving = tall(condensed[pd:])
+    condensed = -apply_tables(coup_tab, lifted, masks)
+    leaving = tall(condensed[pd:], ncomp)
     pl.semaphore_wait(barrier, parts - 1 + nq - 1)
     send_parts(lambda i: ask_send.at[i], lambda i: ask_recv.at[i], 0, 1)
     for j in range(chunks):
-        start_far(0, j, slot_pick, part(leaving, j), 1)
-    for fetch in fetches[7:]:
+        post(0, j, at_slots(slot_pick, part(leaving, j)).reshape(parts, depth, width), 1)
+    for fetch in fetches[8:]:
         fetch.wait()
     stiff = tile_cases(stiff_ref[...])
     red_t = [exact(binv_ref[t], coup_ref[t], TN) for t in range(kinds)]
     schur = [pblock_ref[t] - exact(red_t[t], coup_ref[t], TN) for t in range(kinds)]
-    schur_tab = split(jnp.concatenate(schur, axis=1))
-    red_tab = split(jnp.concatenate(red_t, axis=1))
+    schur = jnp.concatenate(schur, axis=1)
+    near_tab, far_tab = table(schur[:pd]), table(schur[pd:])
+    red_tab = table(jnp.concatenate(red_t, axis=1))
     own = jnp.concatenate([pload_ref[:, k, :] for k in range(ncase)], axis=0)
-    own = own + pick(tall(condensed[:pd]), near_out)
+    own = own + pick(tall(condensed[:pd], ncomp), near_out)
     wait_on(ask_recv.at[rest], part_rsem.at[0])
-    asked = ask_recv[...].reshape(parts, ncomp)
-    asked = jnp.concatenate([asked] * (ncomp // parts), axis=0).T
+    asked = ask_recv[...].reshape(parts, 3 * ncomp)
+    ports = jnp.concatenate([asked[:, 0:ncomp]] * (ncomp // parts), axis=0).T
     port_lane = lax.broadcasted_iota(jnp.int32, (depth, nport), 1).astype(F32)
     asked_pick = jnp.concatenate(
-        [jnp.where(asked[0:depth, i:i + 1] == port_lane, 1.0, 0.0) for i in range(parts)], axis=0
+        [jnp.where(ports[0:depth, i:i + 1] - 1.0 == port_lane, 1.0, 0.0) for i in range(parts)],
+        axis=0,
     ).astype(BF16)
 
-    def arrive(e, own, onward):
-        pieces = []
-        for j in range(chunks):
-            piece = part(own, j) + finish_far(e, j, asked_pick)
-            if onward:
-                start_far(e + 1, j, asked_pick, piece, -1)
-            pieces.append(piece)
-        return jnp.concatenate(pieces, axis=0)
-
-    def operate(e, near, between):
-        cuts = [0, ((chunks - 1) * width) // pd, ncase] if chunks > 1 else [0, ncase]
-        far, near_y, far_y, sent, have = None, None, None, 0, 0
+    def slot_line(r):
+        return jnp.concatenate(
+            [asked[i:i + 1, r * ncomp:r * ncomp + depth] for i in range(parts)], axis=1
+        )
+
+    slot_masks = kind_masks(slot_line(1))
+    slot_stiff = tile_cases(slot_line(2))
+    both_picks = jnp.concatenate([asked_pick, near_slots], axis=0)
+
+    def scatter(e, j, piece):
+        out = at_slots(both_picks, piece)
+        post(e, j, out[:slots].reshape(parts, depth, width), -1)
+        post(e + 1, j, out[slots:].reshape(parts, depth, width), 1)
+
+    def join(a, b):
+        return b if a is None else jnp.concatenate([a, b], axis=0)
+
+    def operate(e, field, onward, between):
+        near = pick(field, near_in)
+        cuts = [0] + [((j + 1) * width) // pd for j in range(chunks)]
+        far, far_at, near_at, image, have, sent = None, None, None, None, 0, 0
         for a, b in zip(cuts[:-1], cuts[1:]):
             if b == ncase:
                 between()
             while have * width < b * pd:
-                piece = finish_far(e, have, slot_pick)
-                far = piece if far is None else jnp.concatenate([far, piece], axis=0)
+                far = join(far, place(take_far(e, have), slot_pick))
+                far_at = join(far_at, far_send[e, have].reshape(slots, width).T)
+                near_at = join(near_at, take_far(e + 1, have))
                 have += 1
             rows = slice(a * pd, b * pd)
             ends = jnp.concatenate([wide(near[rows], pd), wide(far[rows], pd)], axis=0)
-            y = apply_tables(schur_tab, ends) * stiff[:, a * ncomp:b * ncomp]
-            out = tall(y[pd:])
-            far_y = out if far_y is None else jnp.concatenate([far_y, out], axis=0)
-            out = tall(y[:pd])
-            near_y = out if near_y is None else jnp.concatenate([near_y, out], axis=0)
-            while (sent + 1) * width <= b * pd:
-                start_far(e + 1, sent, slot_pick, part(far_y, sent), 1)
+            y = apply_tables(near_tab, ends, masks) * stiff[:, a * ncomp:b * ncomp]
+            done = pick(tall(y, ncomp), near_out)
+            ends = jnp.concatenate([wide(near_at[rows], pd), wide(far_at[rows], pd)], axis=0)
+            y = apply_tables(far_tab, ends, slot_masks) * slot_stiff[:, a * slots:b * slots]
+            image = join(image, done + place(tall(y, slots), asked_pick))
+            while onward and (sent + 1) * width <= b * pd:
+                scatter(e + 2, sent, part(image, sent))
                 sent += 1
-        return far, far_y, pick(near_y, near_out)
-
-    base = arrive(0, own, True)
+        return far, image
+
+    base = None
+    for j in range(chunks):
+        piece = part(own, j) + place(take_far(0, j), asked_pick)
+        scatter(1, j, piece)
+        base = join(base, piece)
     publish(0, base)
-    far_base, _, own = operate(1, pick(base, near_in), lambda: forward(0))
+    far_base, first = operate(1, base, True, lambda: forward(0))
+    publish(1, first)
     publish(3, far_base)
-    first = arrive(2, own, True)
-    publish(1, first)
-    near = pick(first, near_in)
-    forward(3)
-    collect(0)
-    far_first, far_image, own = operate(3, near, lambda: forward(1))
+
+    def grams_of_two():
+        forward(1)
+        collect(0)
+        collect(1)
+        pair = field_rows(0, 2)
+        square = exact(pair, pair, NT)
+        start_gram(
+            jnp.concatenate(
+                [
+                    square[0:allcase, 0:allcase],
+                    square[0:allcase, allcase:],
+                    square[allcase:, allcase:],
+                ],
+                axis=0,
+            )
+        )
+        forward(3)
+
+    far_first, second = operate(3, first, False, grams_of_two)
     publish(4, far_first)
-    collect(1)
-    pair = field_rows(0, 2)
-    square = exact(pair, pair, NT)
-    start_gram(
-        jnp.concatenate(
-            [
-                square[0:allcase, 0:allcase],
-                square[0:allcase, allcase:],
-                square[allcase:, allcase:],
-            ],
-            axis=0,
-        )
-    )
-    near_curve = exact(image_rows(0, own), field_rows(1), NT)
-    far_lines = image_rows(1, far_image)
-    second = arrive(4, own, False)
     publish(2, second)
-    forward(4)
-    collect(4)
+    second_rows = jnp.concatenate([gath[2, my_c, d] for d in range(pd)], axis=1)
 
     n = allcase
-    curve = near_curve + exact(far_lines, field_rows(4), NT)
+    curve = exact(second_rows, field_rows(1), NT)
     curve = jnp.concatenate([curve, jnp.zeros((ncase, 128 - n), F32)], axis=1)
     curve_send[...] = curve
     curve_recv[0] = curve
@@ -416,7 +445,6 @@
     g01 = sym(grams[n:2 * n])
     g11 = sym(grams[2 * n:3 * n])
     both = gauss_solve(g01, jnp.concatenate([g00, g11], axis=1))
-    forward(2)
     image_both = exact(g11, both)
     mine = jnp.where(
         lax.broadcasted_iota(jnp.int32, (n, ncase), 0)
@@ -426,6 +454,7 @@
     )
     chosen = exact(jnp.concatenate([image_both[:, 0:n] - g01, both[:, 0:n]], axis=0), mine)
 
+    forward(4)
     wait_on(curve_recv.at[rest], part_rsem.at[2])
     total = jnp.sum(curve_recv[...], axis=0)
     curve_mine[...] = total
@@ -433,6 +462,7 @@
     for i in range(1, nq):
         send_case(5, curve_mine, curve_all.at[my_c], i, i)
     collect(3)
+    forward(2)
     for i in range(1, nq):
         wait_on(curve_all.at[case_from(i)], case_rsem.at[5, i])
     g12 = curve_all[...].reshape(n, 128)[:, 0:n]
@@ -450,6 +480,7 @@
     answer_rows = mix(0)
     for d in range(pd):
         sol_ref[d] = answer_rows[:, d * nport:(d + 1) * nport]
+    collect(4)
     far_rows = mix(3)
     for d in range(pd):
         nat_far[d] = far_rows[:, d * nport:(d + 1) * nport]
@@ -459,7 +490,7 @@
         [near, jnp.concatenate([nat_far[:, k, :] for k in range(ncase)], axis=1)], axis=0
     )
     scaled = inv_keep[...] / stiff
-    back = scaled - apply_tables(red_tab, ends)
+    back = scaled - apply_tables(red_tab, ends, masks)
     for k in range(ncase):
         bub_ref[:, k, :] = back[:, k * ncomp:(k + 1) * ncomp]
     collect(2)
@@ -543,12 +574,11 @@
             pltpu.VMEM(bubble_inverse.shape, F32),
             pltpu.VMEM((kinds, modes, 2 * pd), F32),
             pltpu.VMEM(port_block.shape, F32),
-            pltpu.VMEM((parts, 1, ncomp), F32),
-            pltpu.VMEM((parts, 1, ncomp), F32),
+            pltpu.VMEM((parts, 1, 3 * ncomp), F32),
+            pltpu.VMEM((parts, 1, 3 * ncomp), F32),
             pltpu.VMEM((5, chunks, parts, depth, width), F32),
             pltpu.VMEM((5, chunks, parts, depth, width), F32),
             pltpu.VMEM((5, nq, pd, ncase, nport), F32),
-            pltpu.VMEM((2, pd, ncase, nport), F32),
             pltpu.VMEM((5 * allcase, pd * nport), F32),
             pltpu.VMEM((8, 3 * allcase * allcase // 8), F32),
             pltpu.VMEM((parts, 8, 3 * allcase * allcase // 8), F32),

time: 62.2 us -> 62.8 us (level)
  Pallas kernels: 61.2 us -> 61.9 us
    pallas_call x1, Pallas kernels: 60.4 us -> 61 us  [local(): pl.pallas_call(body, out_shape=shapes, in_specs=[hbm] * 10, out_specs=(vm...]
where the time goes in v3:
time: 62.8 us; the launch traced here: 62.7 us
  Pallas kernels  61.9 us (99%)
  between operations  0.8 us (1%)
    pallas_call x1, Pallas kernels, local(): pl.pallas_call(body, out_shape=shapes, in_specs=[hbm] * 10, out_specs=(vm...  61 us

profile of v3, /device:TPU:0, one launch (start us, length us, event | category | flops | bytes accessed | tf_op | source)
XLA Modules:
  0.0 62.7 jit_solution(5548537021032248297)
XLA Ops:
  0.6 61.0 %condensed_solve.1 = (f32[48,8,128]{2,1,0:T(8,128)S(1)}, f32[48,8,128]{2,1,0:T(8,128)S(1)}, f32[64,8,128]{2,1,0:T(8,128)S(1)}) custom-call(s32[1,128]{1,0:T(1,128)} %bitcast.7, s32[1,128]{1,0:T(1,128)} %bitcast.8, s32[1,128]{1,0:T(1,128)} %bitcast.9, s32[1,128]{1,0:T(1,128)} %bitcast.10, f32[1,128]{1,0:T(1,128)} %bitcast.11, f32[64,8,128]{2,1,0:T(8,128)} %refs_5_.1, ...), custom_call_target="tpu_custom_call" | custom-call | tf_op jit(solution)/shard_map/condensed_solve/pallas_call | solution.py:561
  61.7 0.9 %emit.1 = (f32[48,8,128]{2,1,0:T(8,128)}, f32[48,8,128]{2,1,0:T(8,128)}, f32[64,8,128]{2,1,0:T(8,128)}) custom-call(f32[48,8,128]{2,1,0:T(8,128)S(1)} %get-tuple-element.6.refs_0_, f32[48,8,128]{2,1,0:T(8,128)S(1)} %get-tuple-element.7.refs_1_, f32[64,8,128]{2,1,0:T(8,128)S(1)} %get-tuple-element.8.refs_2_), custom_call_target="tpu_custom_call" | custom-call | tf_op jit(solution)/shard_map/emit/pallas_call | solution.py:618

commit v4 on v3

--- a/solution.py
+++ b/solution.py
@@ -74,13 +74,12 @@
     far_send,
     far_recv,
     gath,
+    bent_rows,
     rows_all,
+    block_mine,
+    block_case,
     pair_send,
     pair_recv,
-    curve_send,
-    curve_recv,
-    curve_mine,
-    curve_all,
     inv_keep,
     nat_far,
     in_sem,
@@ -256,7 +255,7 @@
         top, low = split(x)
         return mm(top, onehot) + mm(low, onehot)
 
-    def take_far(e, j):
+    def take(e, j):
         wait_on(far_recv.at[e, j, rest], part_rsem.at[3 + e * chunks + j])
         return far_recv[e, j].reshape(slots, width).T
 
@@ -305,21 +304,38 @@
     def field_rows(f, count=1):
         return rows_all[f * allcase:(f + count) * allcase, :]
 
-    def start_gram(value):
-        folded = jnp.concatenate(
-            [value[8 * r:8 * r + 8] for r in range(value.shape[0] // 8)], axis=1
-        )
-        pair_send[...] = folded
-        pair_recv[0] = folded
-        send_parts(lambda i: pair_send, lambda i: pair_recv.at[i], 1, 1)
-
-    def finish_gram():
-        wait_on(pair_recv.at[rest], part_rsem.at[1])
-        total = jnp.sum(pair_recv[...], axis=0)
-        return jnp.concatenate(
-            [total[:, allcase * r:allcase * (r + 1)] for r in range(total.shape[1] // allcase)],
-            axis=0,
-        )
+    def own_rows(f):
+        return jnp.concatenate([gath[f, my_c, d] for d in range(pd)], axis=1)
+
+    def gram_out(s, block):
+        block = jnp.concatenate([block, jnp.zeros((2 * ncase, 128 - allcase), F32)], axis=1)
+        block_mine[s] = block
+        block_case[s, my_c] = block
+        for i in range(1, nq):
+            send_case(5 + s, block_mine.at[s], block_case.at[s, my_c], i, i)
+
+    def gram_on(s):
+        for i in range(1, nq):
+            wait_on(block_case.at[s, case_from(i)], case_rsem.at[5 + s, i])
+        line = jnp.concatenate([block_case[s, q][:, 0:allcase] for q in range(nq)], axis=1)
+        pair_send[s] = line
+        pair_recv[s, 0] = line
+        send_parts(lambda i: pair_send.at[s], lambda i: pair_recv.at[s, i], 1 + s, 1)
+
+    def gram_in(s):
+        wait_on(pair_recv.at[s, rest], part_rsem.at[1 + s])
+        total = jnp.sum(pair_recv[s], axis=0)
+        grams = []
+        for r in range(2):
+            rows = total[r * ncase:(r + 1) * ncase]
+            grams.append(
+                sym(
+                    jnp.concatenate(
+                        [rows[:, q * allcase:(q + 1) * allcase] for q in range(nq)], axis=0
+                    )
+                )
+            )
+        return grams
 
     def sym(g):
         return 0.5 * (g + g.T)
@@ -345,8 +361,12 @@
     stiff = tile_cases(stiff_ref[...])
     red_t = [exact(binv_ref[t], coup_ref[t], TN) for t in range(kinds)]
     schur = [pblock_ref[t] - exact(red_t[t], coup_ref[t], TN) for t in range(kinds)]
-    schur = jnp.concatenate(schur, axis=1)
-    near_tab, far_tab = table(schur[:pd]), table(schur[pd:])
+
+    def corner(a, b):
+        rows, cols = slice(a * pd, (a + 1) * pd), slice(b * pd, (b + 1) * pd)
+        return table(jnp.concatenate([schur[t][rows, cols] for t in range(kinds)], axis=1))
+
+    nn_tab, nf_tab, fn_tab, ff_tab = corner(0, 0), corner(0, 1), corner(1, 0), corner(1, 1)
     red_tab = table(jnp.concatenate(red_t, axis=1))
     own = jnp.concatenate([pload_ref[:, k, :] for k in range(ncase)], axis=0)
     own = own + pick(tall(condensed[:pd], ncomp), near_out)
@@ -371,103 +391,116 @@
     def scatter(e, j, piece):
         out = at_slots(both_picks, piece)
         post(e, j, out[:slots].reshape(parts, depth, width), -1)
-        post(e + 1, j, out[slots:].reshape(parts, depth, width), 1)
+        return lambda: post(e + 1, j, out[slots:].reshape(parts, depth, width), 1)
 
     def join(a, b):
         return b if a is None else jnp.concatenate([a, b], axis=0)
 
-    def operate(e, field, onward, between):
-        near = pick(field, near_in)
-        cuts = [0] + [((j + 1) * width) // pd for j in range(chunks)]
-        far, far_at, near_at, image, have, sent = None, None, None, None, 0, 0
-        for a, b in zip(cuts[:-1], cuts[1:]):
-            if b == ncase:
-                between()
-            while have * width < b * pd:
-                far = join(far, place(take_far(e, have), slot_pick))
-                far_at = join(far_at, far_send[e, have].reshape(slots, width).T)
-                near_at = join(near_at, take_far(e + 1, have))
-                have += 1
-            rows = slice(a * pd, b * pd)
-            ends = jnp.concatenate([wide(near[rows], pd), wide(far[rows], pd)], axis=0)
-            y = apply_tables(near_tab, ends, masks) * stiff[:, a * ncomp:b * ncomp]
-            done = pick(tall(y, ncomp), near_out)
-            ends = jnp.concatenate([wide(near_at[rows], pd), wide(far_at[rows], pd)], axis=0)
-            y = apply_tables(far_tab, ends, slot_masks) * slot_stiff[:, a * slots:b * slots]
-            image = join(image, done + place(tall(y, slots), asked_pick))
-            while onward and (sent + 1) * width <= b * pd:
-                scatter(e + 2, sent, part(image, sent))
-                sent += 1
-        return far, image
+    def near_side(tab, x, a, b):
+        return apply_tables(tab, wide(x, pd), masks) * stiff[:, a * ncomp:b * ncomp]
+
+    def far_side(tab, x, a, b):
+        return apply_tables(tab, wide(x, pd), slot_masks) * slot_stiff[:, a * slots:b * slots]
+
+    def near_ports(y):
+        return pick(tall(y, ncomp), near_out)
+
+    def far_ports(y):
+        return place(tall(y, slots), asked_pick)
+
+    def diagonal(e, field):
+        y_near = near_side(nn_tab, pick(field, near_in), 0, ncase)
+        far_at = [far_send[e, j].reshape(slots, width).T for j in range(chunks)]
+        return y_near, far_side(ff_tab, jnp.concatenate(far_at, axis=0), 0, ncase)
+
+    def take_far_values(e, j):
+        return place(take(e, j), slot_pick)
+
+    cuts = [0] + [((j + 1) * width) // pd for j in range(chunks)]
 
     base = None
     for j in range(chunks):
-        piece = part(own, j) + place(take_far(0, j), asked_pick)
-        scatter(1, j, piece)
+        piece = part(own, j) + place(take(0, j), asked_pick)
+        scatter(1, j, piece)()
         base = join(base, piece)
     publish(0, base)
-    far_base, first = operate(1, base, True, lambda: forward(0))
+
+    y_near, y_far = diagonal(1, base)
+    far_base, near_at, first, sent = None, None, None, 0
+    for j in range(chunks):
+        a, b = cuts[j], cuts[j + 1]
+        if j == chunks - 1:
+            forward(0)
+        far_base = join(far_base, take_far_values(1, j))
+        near_at = join(near_at, take(2, j))
+        rows = slice(a * pd, b * pd)
+        y = y_near[:, a * ncomp:b * ncomp] + near_side(nf_tab, far_base[rows], a, b)
+        done = near_ports(y)
+        y = y_far[:, a * slots:b * slots] + far_side(fn_tab, near_at[rows], a, b)
+        first = join(first, done + far_ports(y))
+        later = []
+        while (sent + 1) * width <= b * pd:
+            later.append(scatter(3, sent, part(first, sent)))
+            sent += 1
+        for post_near in later:
+            post_near()
     publish(1, first)
+
+    y_near, y_far = diagonal(3, first)
+    straight = near_ports(y_near) + far_ports(y_far)
+    collect(0)
+    gram_out(0, exact(jnp.concatenate([own_rows(0), own_rows(1)], axis=0), field_rows(0), NT))
     publish(3, far_base)
-
-    def grams_of_two():
-        forward(1)
-        collect(0)
-        collect(1)
-        pair = field_rows(0, 2)
-        square = exact(pair, pair, NT)
-        start_gram(
-            jnp.concatenate(
-                [
-                    square[0:allcase, 0:allcase],
-                    square[0:allcase, allcase:],
-                    square[allcase:, allcase:],
-                ],
-                axis=0,
-            )
-        )
-        forward(3)
-
-    far_first, second = operate(3, first, False, grams_of_two)
+    far_first, crossed = None, None
+    for j in range(chunks):
+        a, b = cuts[j], cuts[j + 1]
+        if j == chunks - 1:
+            gram_on(0)
+        far_first = join(far_first, take_far_values(3, j))
+        crossed = join(crossed, near_ports(near_side(nf_tab, far_first[a * pd:b * pd], a, b)))
+        if j == 0:
+            forward(1)
+    collect(1)
+    bent = straight + 2.0 * crossed
+    for k in range(ncase):
+        bent_rows[:, k, :] = bent[k * pd:(k + 1) * pd]
+    lines = jnp.concatenate([bent_rows[d] for d in range(pd)], axis=1)
+    gram_out(1, exact(jnp.concatenate([own_rows(1), lines], axis=0), field_rows(1), NT))
     publish(4, far_first)
+    second, near_at = None, None
+    for j in range(chunks):
+        a, b = cuts[j], cuts[j + 1]
+        if j == chunks - 1:
+            forward(3)
+            gram_on(1)
+        near_at = join(near_at, take(4, j))
+        second = join(second, far_ports(far_side(fn_tab, near_at[a * pd:b * pd], a, b)))
+    second = second + straight + crossed
     publish(2, second)
-    second_rows = jnp.concatenate([gath[2, my_c, d] for d in range(pd)], axis=1)
 
     n = allcase
-    curve = exact(second_rows, field_rows(1), NT)
-    curve = jnp.concatenate([curve, jnp.zeros((ncase, 128 - n), F32)], axis=1)
-    curve_send[...] = curve
-    curve_recv[0] = curve
-    send_parts(lambda i: curve_send, lambda i: curve_recv.at[i], 2, 1)
-
-    grams = finish_gram()
-    g00 = sym(grams[0:n])
-    g01 = sym(grams[n:2 * n])
-    g11 = sym(grams[2 * n:3 * n])
-    both = gauss_solve(g01, jnp.concatenate([g00, g11], axis=1))
-    image_both = exact(g11, both)
+    g00, g01 = gram_in(0)
+    eye = jnp.where(
+        lax.broadcasted_iota(jnp.int32, (n, n), 0) == lax.broadcasted_iota(jnp.int32, (n, n), 1),
+        1.0,
+        0.0,
+    )
+    both = gauss_solve(g01, jnp.concatenate([g00, eye], axis=1))
     mine = jnp.where(
         lax.broadcasted_iota(jnp.int32, (n, ncase), 0)
         == lax.broadcasted_iota(jnp.int32, (n, ncase), 1) + my_c * ncase,
         1.0,
         0.0,
     )
-    chosen = exact(jnp.concatenate([image_both[:, 0:n] - g01, both[:, 0:n]], axis=0), mine)
-
+    chosen = exact(jnp.concatenate([both[:, 0:n], g01], axis=0), mine)
+    first_step, g01_mine, inverse = chosen[0:n], chosen[n:2 * n], both[:, n:2 * n]
     forward(4)
-    wait_on(curve_recv.at[rest], part_rsem.at[2])
-    total = jnp.sum(curve_recv[...], axis=0)
-    curve_mine[...] = total
-    curve_all[my_c] = total
-    for i in range(1, nq):
-        send_case(5, curve_mine, curve_all.at[my_c], i, i)
     collect(3)
-    forward(2)
-    for i in range(1, nq):
-        wait_on(curve_all.at[case_from(i)], case_rsem.at[5, i])
-    g12 = curve_all[...].reshape(n, 128)[:, 0:n]
-    beta = gauss_solve(sym(g12) - sym(image_both[:, n:2 * n]), chosen[0:n])
-    alpha = chosen[n:2 * n] + exact(both[:, n:2 * n], beta)
+    g11, g12 = gram_in(1)
+    over = exact(inverse, g11)
+    side = exact(g11, jnp.concatenate([over, first_step], axis=1))
+    beta = gauss_solve(g12 - sym(side[:, 0:n]), side[:, n:] - g01_mine)
+    alpha = first_step + exact(over, beta)
     coefs = jnp.concatenate([alpha, -beta], axis=0).T
     ctop, clow = split(coefs)
     stack = jnp.concatenate([ctop, clow], axis=0)
@@ -481,6 +514,7 @@
     for d in range(pd):
         sol_ref[d] = answer_rows[:, d * nport:(d + 1) * nport]
     collect(4)
+    forward(2)
     far_rows = mix(3)
     for d in range(pd):
         nat_far[d] = far_rows[:, d * nport:(d + 1) * nport]
@@ -502,13 +536,14 @@
     for e in range(5):
         for j in range(chunks):
             wait_on(far_send.at[e, j, rest], part_ssem.at[3 + e * chunks + j])
-    wait_on(pair_recv.at[rest], part_ssem.at[1])
-    wait_on(curve_recv.at[rest], part_ssem.at[2])
+    for s in range(2):
+        wait_on(pair_recv.at[s, rest], part_ssem.at[1 + s])
     for f in range(5):
         for i in range(1, nq):
             wait_on(gath.at[f, my_c], case_ssem.at[f, i])
-    for i in range(1, nq):
-        wait_on(curve_mine, case_ssem.at[5, i])
+    for s in range(2):
+        for i in range(1, nq):
+            wait_on(block_mine.at[s], case_ssem.at[5 + s, i])
 
 
 def emit(*refs):
@@ -579,20 +614,19 @@
             pltpu.VMEM((5, chunks, parts, depth, width), F32),
             pltpu.VMEM((5, chunks, parts, depth, width), F32),
             pltpu.VMEM((5, nq, pd, ncase, nport), F32),
+            pltpu.VMEM((pd, ncase, nport), F32),
             pltpu.VMEM((5 * allcase, pd * nport), F32),
-            pltpu.VMEM((8, 3 * allcase * allcase // 8), F32),
-            pltpu.VMEM((parts, 8, 3 * allcase * allcase // 8), F32),
-            pltpu.VMEM((ncase, 128), F32),
-            pltpu.VMEM((parts, ncase, 128), F32),
-            pltpu.VMEM((ncase, 128), F32),
-            pltpu.VMEM((nq, ncase, 128), F32),
+            pltpu.VMEM((2, 2 * ncase, 128), F32),
+            pltpu.VMEM((2, nq, 2 * ncase, 128), F32),
+            pltpu.VMEM((2, 2 * ncase, nq * allcase), F32),
+            pltpu.VMEM((2, parts, 2 * ncase, nq * allcase), F32),
             pltpu.VMEM((modes, ncase * ncomp), F32),
             pltpu.VMEM((pd, ncase, nport), F32),
             pltpu.SemaphoreType.DMA((10,)),
             pltpu.SemaphoreType.DMA((3 + 5 * chunks,)),
             pltpu.SemaphoreType.DMA((3 + 5 * chunks,)),
-            pltpu.SemaphoreType.DMA((6, nq)),
-            pltpu.SemaphoreType.DMA((6, nq)),
+            pltpu.SemaphoreType.DMA((7, nq)),
+            pltpu.SemaphoreType.DMA((7, nq)),
         ],
         compiler_params=pltpu.CompilerParams(
             collective_id=0, has_side_effects=True, vmem_limit_bytes=32 * 1024 * 1024

time: 62.8 us -> 55.9 us (0.89)
  Pallas kernels: 61.9 us -> 55 us
    pallas_call x1, Pallas kernels: 61 us -> 54.1 us  [local(): pl.pallas_call(body, out_shape=shapes, in_specs=[hbm] * 10, out_specs=(vm...]
where the time goes in v4:
time: 55.9 us; the launch traced here: 55.8 us
  Pallas kernels  55 us (98%)
  between operations  0.8 us (1%)
    pallas_call x1, Pallas kernels, local(): pl.pallas_call(body, out_shape=shapes, in_specs=[hbm] * 10, out_specs=(vm...  54.1 us

profile of v4, /device:TPU:0, one launch (start us, length us, event | category | flops | bytes accessed | tf_op | source)
XLA Modules:
  0.0 55.8 jit_solution(13123783304645373832)
XLA Ops:
  0.6 54.1 %condensed_solve.1 = (f32[48,8,128]{2,1,0:T(8,128)S(1)}, f32[48,8,128]{2,1,0:T(8,128)S(1)}, f32[64,8,128]{2,1,0:T(8,128)S(1)}) custom-call(s32[1,128]{1,0:T(1,128)} %bitcast.7, s32[1,128]{1,0:T(1,128)} %bitcast.8, s32[1,128]{1,0:T(1,128)} %bitcast.9, s32[1,128]{1,0:T(1,128)} %bitcast.10, f32[1,128]{1,0:T(1,128)} %bitcast.11, f32[64,8,128]{2,1,0:T(8,128)} %refs_5_.1, ...), custom_call_target="tpu_custom_call" | custom-call | tf_op jit(solution)/shard_map/condensed_solve/pallas_call | solution.py:596
  54.8 0.9 %emit.1 = (f32[48,8,128]{2,1,0:T(8,128)}, f32[48,8,128]{2,1,0:T(8,128)}, f32[64,8,128]{2,1,0:T(8,128)}) custom-call(f32[48,8,128]{2,1,0:T(8,128)S(1)} %get-tuple-element.6.refs_0_, f32[48,8,128]{2,1,0:T(8,128)S(1)} %get-tuple-element.7.refs_1_, f32[64,8,128]{2,1,0:T(8,128)S(1)} %get-tuple-element.8.refs_2_), custom_call_target="tpu_custom_call" | custom-call | tf_op jit(solution)/shard_map/emit/pallas_call | solution.py:652

commit v5 on v4

--- a/solution.py
+++ b/solution.py
@@ -75,11 +75,10 @@
     far_recv,
     gath,
     bent_rows,
-    rows_all,
-    block_mine,
-    block_case,
-    pair_send,
-    pair_recv,
+    rows_top,
+    rows_low,
+    gram_send,
+    gram_recv,
     inv_keep,
     nat_far,
     in_sem,
@@ -87,8 +86,10 @@
     part_rsem,
     case_ssem,
     case_rsem,
+    gram_ssem,
+    gram_rsem,
 ):
-    parts, npy, nq, depth, width, chunks = sizes
+    parts, npy, nq, depth, width, chunks, fold = sizes
     my_x, my_y, my_c = lax.axis_index("px"), lax.axis_index("py"), lax.axis_index("case")
     me = my_x * npy + my_y
 
@@ -112,13 +113,30 @@
 
     barrier = pltpu.get_barrier_semaphore()
 
-    def greet_part(i, _):
-        pl.semaphore_signal(barrier, inc=1, device_id=part_id(i), device_id_type=MESH)
-        return 0
-
-    lax.fori_loop(1, parts, greet_part, 0)
-    for i in range(1, nq):
-        pl.semaphore_signal(barrier, inc=1, device_id=case_id(i), device_id_type=MESH)
+    order = sorted(range(1, parts), key=lambda i: -min(i % npy, npy - i % npy))
+
+    def each_other(act):
+        def per_part(i, _):
+            for q in reversed(range(nq)):
+                act(i, q)
+            return 0
+
+        if parts <= 8:
+            for i in order:
+                per_part(i, 0)
+        else:
+            lax.fori_loop(1, parts, per_part, 0)
+        for q in reversed(range(1, nq)):
+            act(0, q)
+
+    def device(i, q):
+        x, y, _ = part_id(i)
+        return (x, y, case_to(q))
+
+    def greet(i, q):
+        pl.semaphore_signal(barrier, inc=1, device_id=device(i, q), device_id_type=MESH)
+
+    each_other(greet)
 
     inputs = (
         (near_hbm, near_ref),
@@ -181,8 +199,6 @@
     near_out = jnp.where(lane.astype(F32) == as_column(near_row), 1.0, 0.0).astype(BF16)
     near_slots = lax.dot_general(slot_pick, near_in, NT, preferred_element_type=F32).astype(BF16)
 
-    order = sorted(range(1, parts), key=lambda i: -min(i % npy, npy - i % npy))
-
     def send_parts(src, dst, e, sign):
         def body(i, _):
             pltpu.make_async_remote_copy(
@@ -256,14 +272,14 @@
         return mm(top, onehot) + mm(low, onehot)
 
     def take(e, j):
-        wait_on(far_recv.at[e, j, rest], part_rsem.at[3 + e * chunks + j])
+        wait_on(far_recv.at[e, j, rest], part_rsem.at[1 + e * chunks + j])
         return far_recv[e, j].reshape(slots, width).T
 
     def post(e, j, out, sign):
         far_send[e, j] = out
         far_recv[e, j, 0] = out[0]
         send_parts(
-            lambda i: far_send.at[e, j, i], lambda i: far_recv.at[e, j, i], 3 + e * chunks + j, sign
+            lambda i: far_send.at[e, j, i], lambda i: far_recv.at[e, j, i], 1 + e * chunks + j, sign
         )
 
     def send_case(f, src, dst, sem, step):
@@ -295,47 +311,57 @@
 
         def body(d, _):
             cols = pl.ds(pl.multiple_of(d * nport, nport), nport)
-            for q in range(nq):
-                rows_all[pl.ds(f * allcase + q * ncase, ncase), cols] = gath[f, q, d]
+            block = jnp.concatenate([gath[f, q, d] for q in range(nq)], axis=0)
+            top, low = split(block)
+            rows_top[f * allcase:(f + 1) * allcase, cols] = top
+            rows_low[f * allcase:(f + 1) * allcase, cols] = low
             return 0
 
         lax.fori_loop(0, pd, body, 0, unroll=4)
 
-    def field_rows(f, count=1):
-        return rows_all[f * allcase:(f + count) * allcase, :]
+    def against(x, f):
+        top, low = split(x)
+        band = slice(f * allcase, (f + 1) * allcase)
+        lead = lax.dot_general(
+            jnp.concatenate([top, low], axis=0),
+            rows_top[band, :],
+            NT,
+            preferred_element_type=F32,
+        )
+        rest = lax.dot_general(top, rows_low[band, :], NT, preferred_element_type=F32)
+        return lead[:x.shape[0]] + lead[x.shape[0]:] + rest
 
     def own_rows(f):
         return jnp.concatenate([gath[f, my_c, d] for d in range(pd)], axis=1)
 
     def gram_out(s, block):
-        block = jnp.concatenate([block, jnp.zeros((2 * ncase, 128 - allcase), F32)], axis=1)
-        block_mine[s] = block
-        block_case[s, my_c] = block
-        for i in range(1, nq):
-            send_case(5 + s, block_mine.at[s], block_case.at[s, my_c], i, i)
-
-    def gram_on(s):
-        for i in range(1, nq):
-            wait_on(block_case.at[s, case_from(i)], case_rsem.at[5 + s, i])
-        line = jnp.concatenate([block_case[s, q][:, 0:allcase] for q in range(nq)], axis=1)
-        pair_send[s] = line
-        pair_recv[s, 0] = line
-        send_parts(lambda i: pair_send.at[s], lambda i: pair_recv.at[s, i], 1 + s, 1)
+        high = ncase // fold
+        folded = jnp.concatenate([block[r * high:(r + 1) * high] for r in range(fold)], axis=1)
+        gram_send[s] = folded
+        gram_recv[s, my_c * parts] = folded
+
+        def send(i, q):
+            pltpu.make_async_remote_copy(
+                src_ref=gram_send.at[s],
+                dst_ref=gram_recv.at[s, my_c * parts + i],
+                send_sem=gram_ssem.at[s],
+                recv_sem=gram_rsem.at[s],
+                device_id=device(i, q),
+                device_id_type=MESH,
+            ).start()
+
+        each_other(send)
+
+    others = pl.ds(1, nq * parts - 1)
 
     def gram_in(s):
-        wait_on(pair_recv.at[s, rest], part_rsem.at[1 + s])
-        total = jnp.sum(pair_recv[s], axis=0)
-        grams = []
-        for r in range(2):
-            rows = total[r * ncase:(r + 1) * ncase]
-            grams.append(
-                sym(
-                    jnp.concatenate(
-                        [rows[:, q * allcase:(q + 1) * allcase] for q in range(nq)], axis=0
-                    )
-                )
-            )
-        return grams
+        wait_on(gram_recv.at[s, others], gram_rsem.at[s])
+        lines = []
+        for q in range(nq):
+            total = jnp.sum(gram_recv[s, q * parts:(q + 1) * parts], axis=0)
+            for r in range(fold):
+                lines.append(total[:, r * allcase:(r + 1) * allcase])
+        return sym(jnp.concatenate(lines, axis=0))
 
     def sym(g):
         return 0.5 * (g + g.T)
@@ -347,14 +373,20 @@
         fetch.wait()
     inv_tab = table(jnp.concatenate([binv_ref[t] for t in range(kinds)], axis=1))
     coup_tab = table(jnp.concatenate([coup_ref[t].T for t in range(kinds)], axis=1))
-    loads = jnp.concatenate([bload_ref[:, k, :] for k in range(ncase)], axis=1)
-    lifted = apply_tables(inv_tab, loads, masks)
-    inv_keep[...] = lifted
-    condensed = -apply_tables(coup_tab, lifted, masks)
-    leaving = tall(condensed[pd:], ncomp)
-    pl.semaphore_wait(barrier, parts - 1 + nq - 1)
-    send_parts(lambda i: ask_send.at[i], lambda i: ask_recv.at[i], 0, 1)
+    ready = [0] + [-(-((j + 1) * width) // pd) for j in range(chunks)]
+    condensed_near, leaving = [], None
     for j in range(chunks):
+        a, b = ready[j], ready[j + 1]
+        loads = jnp.concatenate([bload_ref[:, k, :] for k in range(a, b)], axis=1)
+        lifted = apply_tables(inv_tab, loads, masks)
+        inv_keep[:, a * ncomp:b * ncomp] = lifted
+        condensed = -apply_tables(coup_tab, lifted, masks)
+        condensed_near.append(tall(condensed[:pd], ncomp))
+        out = tall(condensed[pd:], ncomp)
+        leaving = out if leaving is None else jnp.concatenate([leaving, out], axis=0)
+        if j == 0:
+            pl.semaphore_wait(barrier, parts * nq - 1)
+            send_parts(lambda i: ask_send.at[i], lambda i: ask_recv.at[i], 0, 1)
         post(0, j, at_slots(slot_pick, part(leaving, j)).reshape(parts, depth, width), 1)
     for fetch in fetches[8:]:
         fetch.wait()
@@ -369,7 +401,7 @@
     nn_tab, nf_tab, fn_tab, ff_tab = corner(0, 0), corner(0, 1), corner(1, 0), corner(1, 1)
     red_tab = table(jnp.concatenate(red_t, axis=1))
     own = jnp.concatenate([pload_ref[:, k, :] for k in range(ncase)], axis=0)
-    own = own + pick(tall(condensed[:pd], ncomp), near_out)
+    own = own + pick(jnp.concatenate(condensed_near, axis=0), near_out)
     wait_on(ask_recv.at[rest], part_rsem.at[0])
     asked = ask_recv[...].reshape(parts, 3 * ncomp)
     ports = jnp.concatenate([asked[:, 0:ncomp]] * (ncomp // parts), axis=0).T
@@ -426,7 +458,7 @@
     publish(0, base)
 
     y_near, y_far = diagonal(1, base)
-    far_base, near_at, first, sent = None, None, None, 0
+    far_base, near_at, first, sent, later = None, None, None, 0, []
     for j in range(chunks):
         a, b = cuts[j], cuts[j + 1]
         if j == chunks - 1:
@@ -438,48 +470,48 @@
         done = near_ports(y)
         y = y_far[:, a * slots:b * slots] + far_side(fn_tab, near_at[rows], a, b)
         first = join(first, done + far_ports(y))
-        later = []
         while (sent + 1) * width <= b * pd:
             later.append(scatter(3, sent, part(first, sent)))
             sent += 1
-        for post_near in later:
-            post_near()
     publish(1, first)
 
     y_near, y_far = diagonal(3, first)
     straight = near_ports(y_near) + far_ports(y_far)
     collect(0)
-    gram_out(0, exact(jnp.concatenate([own_rows(0), own_rows(1)], axis=0), field_rows(0), NT))
+    early = against(jnp.concatenate([own_rows(0), own_rows(1)], axis=0), 0)
+    gram_out(0, early[:ncase])
+    gram_out(1, early[ncase:])
+    for post_near in later:
+        post_near()
     publish(3, far_base)
     far_first, crossed = None, None
     for j in range(chunks):
         a, b = cuts[j], cuts[j + 1]
         if j == chunks - 1:
-            gram_on(0)
+            forward(1)
         far_first = join(far_first, take_far_values(3, j))
         crossed = join(crossed, near_ports(near_side(nf_tab, far_first[a * pd:b * pd], a, b)))
-        if j == 0:
-            forward(1)
     collect(1)
     bent = straight + 2.0 * crossed
     for k in range(ncase):
         bent_rows[:, k, :] = bent[k * pd:(k + 1) * pd]
     lines = jnp.concatenate([bent_rows[d] for d in range(pd)], axis=1)
-    gram_out(1, exact(jnp.concatenate([own_rows(1), lines], axis=0), field_rows(1), NT))
+    late = against(jnp.concatenate([lines, own_rows(1)], axis=0), 1)
+    gram_out(3, late[:ncase])
+    gram_out(2, late[ncase:])
     publish(4, far_first)
     second, near_at = None, None
     for j in range(chunks):
         a, b = cuts[j], cuts[j + 1]
         if j == chunks - 1:
             forward(3)
-            gram_on(1)
         near_at = join(near_at, take(4, j))
         second = join(second, far_ports(far_side(fn_tab, near_at[a * pd:b * pd], a, b)))
     second = second + straight + crossed
     publish(2, second)
 
     n = allcase
-    g00, g01 = gram_in(0)
+    g00, g01 = gram_in(0), gram_in(1)
     eye = jnp.where(
         lax.broadcasted_iota(jnp.int32, (n, n), 0) == lax.broadcasted_iota(jnp.int32, (n, n), 1),
         1.0,
@@ -496,9 +528,19 @@
     first_step, g01_mine, inverse = chosen[0:n], chosen[n:2 * n], both[:, n:2 * n]
     forward(4)
     collect(3)
-    g11, g12 = gram_in(1)
+    g11 = gram_in(2)
     over = exact(inverse, g11)
     side = exact(g11, jnp.concatenate([over, first_step], axis=1))
+    wait_on(ask_send.at[rest], part_ssem.at[0])
+    for e in range(5):
+        for j in range(chunks):
+            wait_on(far_send.at[e, j, rest], part_ssem.at[1 + e * chunks + j])
+    for s in range(4):
+        wait_on(gram_recv.at[s, others], gram_ssem.at[s])
+    for f in (0, 1, 3):
+        for i in range(1, nq):
+            wait_on(gath.at[f, my_c], case_ssem.at[f, i])
+    g12 = gram_in(3)
     beta = gauss_solve(g12 - sym(side[:, 0:n]), side[:, n:] - g01_mine)
     alpha = first_step + exact(over, beta)
     coefs = jnp.concatenate([alpha, -beta], axis=0).T
@@ -506,9 +548,9 @@
     stack = jnp.concatenate([ctop, clow], axis=0)
 
     def mix(f):
-        vtop, vlow = split(field_rows(f, 2))
-        lead = mm(stack, vtop)
-        return lead[0:ncase] + lead[ncase:] + mm(ctop, vlow)
+        band = slice(f * allcase, (f + 2) * allcase)
+        lead = mm(stack, rows_top[band, :])
+        return lead[0:ncase] + lead[ncase:] + mm(ctop, rows_low[band, :])
 
     answer_rows = mix(0)
     for d in range(pd):
@@ -532,18 +574,9 @@
     for d in range(pd):
         res_ref[d] = gath[0, my_c, d] - drop_rows[:, d * nport:(d + 1) * nport]
 
-    wait_on(ask_send.at[rest], part_ssem.at[0])
-    for e in range(5):
-        for j in range(chunks):
-            wait_on(far_send.at[e, j, rest], part_ssem.at[3 + e * chunks + j])
-    for s in range(2):
-        wait_on(pair_recv.at[s, rest], part_ssem.at[1 + s])
-    for f in range(5):
+    for f in (2, 4):
         for i in range(1, nq):
             wait_on(gath.at[f, my_c], case_ssem.at[f, i])
-    for s in range(2):
-        for i in range(1, nq):
-            wait_on(block_mine.at[s], case_ssem.at[5 + s, i])
 
 
 def emit(*refs):
@@ -582,11 +615,12 @@
     allcase = nq * ncase
     width = 128 if (ncase * pd) % 128 == 0 else ncase * pd
     chunks = ncase * pd // width
+    fold = max(1, 128 // allcase)
     vmem = pl.BlockSpec(memory_space=pltpu.VMEM)
     hbm = pl.BlockSpec(memory_space=pltpu.HBM)
 
     def body(*refs):
-        kernel((parts, npy, nq, depth, width, chunks), *refs)
+        kernel((parts, npy, nq, depth, width, chunks, fold), *refs)
 
     shapes = (
         jax.ShapeDtypeStruct(port_load.shape, F32),
@@ -615,18 +649,19 @@
             pltpu.VMEM((5, chunks, parts, depth, width), F32),
             pltpu.VMEM((5, nq, pd, ncase, nport), F32),
             pltpu.VMEM((pd, ncase, nport), F32),
-            pltpu.VMEM((5 * allcase, pd * nport), F32),
-            pltpu.VMEM((2, 2 * ncase, 128), F32),
-            pltpu.VMEM((2, nq, 2 * ncase, 128), F32),
-            pltpu.VMEM((2, 2 * ncase, nq * allcase), F32),
-            pltpu.VMEM((2, parts, 2 * ncase, nq * allcase), F32),
+            pltpu.VMEM((5 * allcase, pd * nport), BF16),
+            pltpu.VMEM((5 * allcase, pd * nport), BF16),
+            pltpu.VMEM((4, ncase // fold, fold * allcase), F32),
+            pltpu.VMEM((4, nq * parts, ncase // fold, fold * allcase), F32),
             pltpu.VMEM((modes, ncase * ncomp), F32),
             pltpu.VMEM((pd, ncase, nport), F32),
             pltpu.SemaphoreType.DMA((10,)),
-            pltpu.SemaphoreType.DMA((3 + 5 * chunks,)),
-            pltpu.SemaphoreType.DMA((3 + 5 * chunks,)),
-            pltpu.SemaphoreType.DMA((7, nq)),
-            pltpu.SemaphoreType.DMA((7, nq)),
+            pltpu.SemaphoreType.DMA((1 + 5 * chunks,)),
+            pltpu.SemaphoreType.DMA((1 + 5 * chunks,)),
+            pltpu.SemaphoreType.DMA((5, nq)),
+            pltpu.SemaphoreType.DMA((5, nq)),
+            pltpu.SemaphoreType.DMA((4,)),
+            pltpu.SemaphoreType.DMA((4,)),
         ],
         compiler_params=pltpu.CompilerParams(
             collective_id=0, has_side_effects=True, vmem_limit_bytes=32 * 1024 * 1024

time: 55.9 us -> 54.3 us (0.971)
  Pallas kernels: 55 us -> 53.3 us
    pallas_call x1, Pallas kernels: 54.1 us -> 52.5 us  [local(): pl.pallas_call(body, out_shape=shapes, in_specs=[hbm] * 10, out_specs=(vm...]
where the time goes in v5:
time: 54.3 us; the launch traced here: 54.2 us
  Pallas kernels  53.3 us (98%)
  between operations  0.8 us (1%)
    pallas_call x1, Pallas kernels, local(): pl.pallas_call(body, out_shape=shapes, in_specs=[hbm] * 10, out_specs=(vm...  52.5 us

profile of v5, /device:TPU:0, one launch (start us, length us, event | category | flops | bytes accessed | tf_op | source)
XLA Modules:
  0.0 54.2 jit_solution(3909868281167159896)
XLA Ops:
  0.6 52.5 %condensed_solve.1 = (f32[48,8,128]{2,1,0:T(8,128)S(1)}, f32[48,8,128]{2,1,0:T(8,128)S(1)}, f32[64,8,128]{2,1,0:T(8,128)S(1)}) custom-call(s32[1,128]{1,0:T(1,128)} %bitcast.7, s32[1,128]{1,0:T(1,128)} %bitcast.8, s32[1,128]{1,0:T(1,128)} %bitcast.9, s32[1,128]{1,0:T(1,128)} %bitcast.10, f32[1,128]{1,0:T(1,128)} %bitcast.11, f32[64,8,128]{2,1,0:T(8,128)} %refs_5_.1, ...), custom_call_target="tpu_custom_call" | custom-call | tf_op jit(solution)/shard_map/condensed_solve/pallas_call | solution.py:630
  53.1 0.9 %emit.1 = (f32[48,8,128]{2,1,0:T(8,128)}, f32[48,8,128]{2,1,0:T(8,128)}, f32[64,8,128]{2,1,0:T(8,128)}) custom-call(f32[48,8,128]{2,1,0:T(8,128)S(1)} %get-tuple-element.6.refs_0_, f32[48,8,128]{2,1,0:T(8,128)S(1)} %get-tuple-element.7.refs_1_, f32[64,8,128]{2,1,0:T(8,128)S(1)} %get-tuple-element.8.refs_2_), custom_call_target="tpu_custom_call" | custom-call | tf_op jit(solution)/shard_map/emit/pallas_call | solution.py:687

commit v6 on v5

--- a/solution.py
+++ b/solution.py
@@ -82,11 +82,9 @@
     inv_keep,
     nat_far,
     in_sem,
-    part_ssem,
+    send_sem,
     part_rsem,
-    case_ssem,
     case_rsem,
-    gram_ssem,
     gram_rsem,
 ):
     parts, npy, nq, depth, width, chunks, fold = sizes
@@ -133,10 +131,13 @@
         x, y, _ = part_id(i)
         return (x, y, case_to(q))
 
-    def greet(i, q):
-        pl.semaphore_signal(barrier, inc=1, device_id=device(i, q), device_id_type=MESH)
-
-    each_other(greet)
+    def greet_part(i, _):
+        pl.semaphore_signal(barrier, inc=1, device_id=part_id(i), device_id_type=MESH)
+        return 0
+
+    lax.fori_loop(1, parts, greet_part, 0)
+    for i in range(1, nq):
+        pl.semaphore_signal(barrier, inc=1, device_id=case_id(i), device_id_type=MESH)
 
     inputs = (
         (near_hbm, near_ref),
@@ -182,29 +183,12 @@
     slot_sub = lax.broadcasted_iota(jnp.int32, (slots, ncomp), 0)
     slot_pick = jnp.where(slot_sub == slot_row, 1.0, 0.0).astype(BF16)
     step_sub = lax.broadcasted_iota(jnp.int32, (parts, ncomp), 0)
-    naming = jnp.concatenate(
-        [
-            jnp.where(step_sub == step_row, row, 0.0)
-            for row in ((far_row + 1).astype(F32), kind_row.astype(F32), stiff_ref[...])
-        ],
-        axis=0,
-    )
-    ranked = jnp.where(sub == rank, 1.0, 0.0)
-    wanted = exact(naming, ranked, NT)
-    wanted = jnp.concatenate([wanted[r * parts:(r + 1) * parts] for r in range(3)], axis=1)
-    wanted = wanted.reshape(parts, 1, 3 * ncomp)
-    ask_send[...] = wanted
-    ask_recv[0] = wanted[0]
-    near_in = jnp.where(sub == near_row, 1.0, 0.0).astype(BF16)
-    near_out = jnp.where(lane.astype(F32) == as_column(near_row), 1.0, 0.0).astype(BF16)
-    near_slots = lax.dot_general(slot_pick, near_in, NT, preferred_element_type=F32).astype(BF16)
-
     def send_parts(src, dst, e, sign):
         def body(i, _):
             pltpu.make_async_remote_copy(
                 src_ref=src(i),
                 dst_ref=dst(i),
-                send_sem=part_ssem.at[e],
+                send_sem=send_sem.at[0 if e else 3],
                 recv_sem=part_rsem.at[e],
                 device_id=part_id(i if sign > 0 else -i),
                 device_id_type=MESH,
@@ -286,7 +270,7 @@
         pltpu.make_async_remote_copy(
             src_ref=src,
             dst_ref=dst,
-            send_sem=case_ssem.at[f, sem],
+            send_sem=send_sem.at[1],
             recv_sem=case_rsem.at[f, sem],
             device_id=case_id(step),
             device_id_type=MESH,
@@ -328,8 +312,14 @@
             NT,
             preferred_element_type=F32,
         )
-        rest = lax.dot_general(top, rows_low[band, :], NT, preferred_element_type=F32)
-        return lead[:x.shape[0]] + lead[x.shape[0]:] + rest
+        low_lead = lax.dot_general(
+            jnp.concatenate([top, low], axis=0),
+            rows_low[band, :],
+            NT,
+            preferred_element_type=F32,
+        )
+        total = lead + low_lead
+        return total[:x.shape[0]] + total[x.shape[0]:]
 
     def own_rows(f):
         return jnp.concatenate([gath[f, my_c, d] for d in range(pd)], axis=1)
@@ -344,7 +334,7 @@
             pltpu.make_async_remote_copy(
                 src_ref=gram_send.at[s],
                 dst_ref=gram_recv.at[s, my_c * parts + i],
-                send_sem=gram_ssem.at[s],
+                send_sem=send_sem.at[2],
                 recv_sem=gram_rsem.at[s],
                 device_id=device(i, q),
                 device_id_type=MESH,
@@ -373,6 +363,22 @@
         fetch.wait()
     inv_tab = table(jnp.concatenate([binv_ref[t] for t in range(kinds)], axis=1))
     coup_tab = table(jnp.concatenate([coup_ref[t].T for t in range(kinds)], axis=1))
+    def ask():
+        naming = jnp.concatenate(
+            [
+                jnp.where(step_sub == step_row, row, 0.0)
+                for row in ((far_row + 1).astype(F32), kind_row.astype(F32), stiff_ref[...])
+            ],
+            axis=0,
+        )
+        ranked = jnp.where(sub == rank, 1.0, 0.0)
+        wanted = exact(naming, ranked, NT)
+        wanted = jnp.concatenate([wanted[r * parts:(r + 1) * parts] for r in range(3)], axis=1)
+        wanted = wanted.reshape(parts, 1, 3 * ncomp)
+        ask_send[...] = wanted
+        ask_recv[0] = wanted[0]
+        send_parts(lambda i: ask_send.at[i], lambda i: ask_recv.at[i], 0, 1)
+
     ready = [0] + [-(-((j + 1) * width) // pd) for j in range(chunks)]
     condensed_near, leaving = [], None
     for j in range(chunks):
@@ -385,11 +391,16 @@
         out = tall(condensed[pd:], ncomp)
         leaving = out if leaving is None else jnp.concatenate([leaving, out], axis=0)
         if j == 0:
-            pl.semaphore_wait(barrier, parts * nq - 1)
-            send_parts(lambda i: ask_send.at[i], lambda i: ask_recv.at[i], 0, 1)
+            pl.semaphore_wait(barrier, parts + nq - 2)
         post(0, j, at_slots(slot_pick, part(leaving, j)).reshape(parts, depth, width), 1)
+        if j == 0:
+            ask()
     for fetch in fetches[8:]:
         fetch.wait()
+    near_in = jnp.where(sub == near_row, 1.0, 0.0).astype(BF16)
+    near_out = jnp.where(lane.astype(F32) == as_column(near_row), 1.0, 0.0).astype(BF16)
+    near_slots = lax.dot_general(slot_pick, near_in, NT, preferred_element_type=F32).astype(BF16)
+
     stiff = tile_cases(stiff_ref[...])
     red_t = [exact(binv_ref[t], coup_ref[t], TN) for t in range(kinds)]
     schur = [pblock_ref[t] - exact(red_t[t], coup_ref[t], TN) for t in range(kinds)]
@@ -500,16 +511,6 @@
     gram_out(3, late[:ncase])
     gram_out(2, late[ncase:])
     publish(4, far_first)
-    second, near_at = None, None
-    for j in range(chunks):
-        a, b = cuts[j], cuts[j + 1]
-        if j == chunks - 1:
-            forward(3)
-        near_at = join(near_at, take(4, j))
-        second = join(second, far_ports(far_side(fn_tab, near_at[a * pd:b * pd], a, b)))
-    second = second + straight + crossed
-    publish(2, second)
-
     n = allcase
     g00, g01 = gram_in(0), gram_in(1)
     eye = jnp.where(
@@ -526,20 +527,21 @@
     )
     chosen = exact(jnp.concatenate([both[:, 0:n], g01], axis=0), mine)
     first_step, g01_mine, inverse = chosen[0:n], chosen[n:2 * n], both[:, n:2 * n]
-    forward(4)
-    collect(3)
+    second, near_at = None, None
+    for j in range(chunks):
+        a, b = cuts[j], cuts[j + 1]
+        if j == chunks - 1:
+            forward(3)
+        near_at = join(near_at, take(4, j))
+        second = join(second, far_ports(far_side(fn_tab, near_at[a * pd:b * pd], a, b)))
+    second = second + straight + crossed
+    publish(2, second)
+
     g11 = gram_in(2)
     over = exact(inverse, g11)
     side = exact(g11, jnp.concatenate([over, first_step], axis=1))
-    wait_on(ask_send.at[rest], part_ssem.at[0])
-    for e in range(5):
-        for j in range(chunks):
-            wait_on(far_send.at[e, j, rest], part_ssem.at[1 + e * chunks + j])
-    for s in range(4):
-        wait_on(gram_recv.at[s, others], gram_ssem.at[s])
-    for f in (0, 1, 3):
-        for i in range(1, nq):
-            wait_on(gath.at[f, my_c], case_ssem.at[f, i])
+    collect(3)
+    forward(4)
     g12 = gram_in(3)
     beta = gauss_solve(g12 - sym(side[:, 0:n]), side[:, n:] - g01_mine)
     alpha = first_step + exact(over, beta)
@@ -574,9 +576,10 @@
     for d in range(pd):
         res_ref[d] = gath[0, my_c, d] - drop_rows[:, d * nport:(d + 1) * nport]
 
-    for f in (2, 4):
-        for i in range(1, nq):
-            wait_on(gath.at[f, my_c], case_ssem.at[f, i])
+    wait_on(far_send.at[:, :, rest], send_sem.at[0])
+    wait_on(gath.at[:, pl.ds(1, nq - 1)], send_sem.at[1])
+    wait_on(gram_recv.at[:, others], send_sem.at[2])
+    wait_on(ask_send.at[rest], send_sem.at[3])
 
 
 def emit(*refs):
@@ -656,11 +659,9 @@
             pltpu.VMEM((modes, ncase * ncomp), F32),
             pltpu.VMEM((pd, ncase, nport), F32),
             pltpu.SemaphoreType.DMA((10,)),
-            pltpu.SemaphoreType.DMA((1 + 5 * chunks,)),
+            pltpu.SemaphoreType.DMA((4,)),
             pltpu.SemaphoreType.DMA((1 + 5 * chunks,)),
             pltpu.SemaphoreType.DMA((5, nq)),
-            pltpu.SemaphoreType.DMA((5, nq)),
-            pltpu.SemaphoreType.DMA((4,)),
             pltpu.SemaphoreType.DMA((4,)),
         ],
         compiler_params=pltpu.CompilerParams(

time: 54.3 us -> 53.8 us (level)
  no operation moved by 1% of the time
where the time goes in v6:
time: 53.8 us; the launch traced here: 53.6 us
  Pallas kernels  53 us (99%)
  between operations  0.64 us (1%)
    pallas_call x1, Pallas kernels, local(): pl.pallas_call(body, out_shape=shapes, in_specs=[hbm] * 10, out_specs=(vm...  52.1 us

profile of v6, /device:TPU:0, one launch (start us, length us, event | category | flops | bytes accessed | tf_op | source)
XLA Modules:
  0.0 53.6 jit_solution(12572365324844299744)
XLA Ops:
  0.6 52.1 %condensed_solve.1 = (f32[48,8,128]{2,1,0:T(8,128)S(1)}, f32[48,8,128]{2,1,0:T(8,128)S(1)}, f32[64,8,128]{2,1,0:T(8,128)S(1)}) custom-call(s32[1,128]{1,0:T(1,128)} %bitcast.7, s32[1,128]{1,0:T(1,128)} %bitcast.8, s32[1,128]{1,0:T(1,128)} %bitcast.9, s32[1,128]{1,0:T(1,128)} %bitcast.10, f32[1,128]{1,0:T(1,128)} %bitcast.11, f32[64,8,128]{2,1,0:T(8,128)} %refs_5_.1, ...), custom_call_target="tpu_custom_call" | custom-call | tf_op jit(solution)/shard_map/condensed_solve/pallas_call | solution.py:633
  52.8 0.9 %emit.1 = (f32[48,8,128]{2,1,0:T(8,128)}, f32[48,8,128]{2,1,0:T(8,128)}, f32[64,8,128]{2,1,0:T(8,128)}) custom-call(f32[48,8,128]{2,1,0:T(8,128)S(1)} %get-tuple-element.6.refs_0_, f32[48,8,128]{2,1,0:T(8,128)S(1)} %get-tuple-element.7.refs_1_, f32[64,8,128]{2,1,0:T(8,128)S(1)} %get-tuple-element.8.refs_2_), custom_call_target="tpu_custom_call" | custom-call | tf_op jit(solution)/shard_map/emit/pallas_call | solution.py:688

commit v7 on v6

--- a/solution.py
+++ b/solution.py
@@ -266,36 +266,47 @@
             lambda i: far_send.at[e, j, i], lambda i: far_recv.at[e, j, i], 1 + e * chunks + j, sign
         )
 
-    def send_case(f, src, dst, sem, step):
+    cuts = [0] + [((j + 1) * width) // pd for j in range(chunks)]
+
+    def span(f, j):
+        if f in (1, 2):
+            return pl.ds(cuts[j] * pd, (cuts[j + 1] - cuts[j]) * pd)
+        return pl.ds(j * width, width)
+
+    def send_case(f, j, block, sem, step):
         pltpu.make_async_remote_copy(
-            src_ref=src,
-            dst_ref=dst,
+            src_ref=block,
+            dst_ref=block,
             send_sem=send_sem.at[1],
-            recv_sem=case_rsem.at[f, sem],
+            recv_sem=case_rsem.at[f, j, sem],
             device_id=case_id(step),
             device_id_type=MESH,
         ).start()
 
-    def publish(f, field):
-        for k in range(ncase):
-            gath[f, my_c, :, k, :] = field[k * pd:(k + 1) * pd]
+    def publish(f, j, rows):
+        gath[f, my_c, span(f, j)] = rows
         for i in reversed(direct):
-            send_case(f, gath.at[f, my_c], gath.at[f, my_c], i, i)
-
-    def forward(f):
+            send_case(f, j, gath.at[f, my_c, span(f, j)], i, i)
+
+    def forward(f, *pieces):
         if nq == 4:
-            block = gath.at[f, case_from(2)]
-            wait_on(block, case_rsem.at[f, 2])
-            send_case(f, block, block, 3, 1)
+            for j in pieces or range(chunks):
+                block = gath.at[f, case_from(2), span(f, j)]
+                wait_on(block, case_rsem.at[f, j, 2])
+                send_case(f, j, block, 3, 1)
+
+    def lines(ref, d):
+        return ref[pl.ds(d, ncase, stride=pd), :]
 
     def collect(f):
         for i in range(1, nq):
             if nq != 4 or i != 2:
-                wait_on(gath.at[f, case_from(i)], case_rsem.at[f, i])
+                for j in range(chunks):
+                    wait_on(gath.at[f, case_from(i), span(f, j)], case_rsem.at[f, j, i])
 
         def body(d, _):
             cols = pl.ds(pl.multiple_of(d * nport, nport), nport)
-            block = jnp.concatenate([gath[f, q, d] for q in range(nq)], axis=0)
+            block = jnp.concatenate([lines(gath.at[f, q], d) for q in range(nq)], axis=0)
             top, low = split(block)
             rows_top[f * allcase:(f + 1) * allcase, cols] = top
             rows_low[f * allcase:(f + 1) * allcase, cols] = low
@@ -322,7 +333,7 @@
         return total[:x.shape[0]] + total[x.shape[0]:]
 
     def own_rows(f):
-        return jnp.concatenate([gath[f, my_c, d] for d in range(pd)], axis=1)
+        return jnp.concatenate([lines(gath.at[f, my_c], d) for d in range(pd)], axis=1)
 
     def gram_out(s, block):
         high = ncase // fold
@@ -346,12 +357,12 @@
 
     def gram_in(s):
         wait_on(gram_recv.at[s, others], gram_rsem.at[s])
-        lines = []
+        rows = []
         for q in range(nq):
             total = jnp.sum(gram_recv[s, q * parts:(q + 1) * parts], axis=0)
             for r in range(fold):
-                lines.append(total[:, r * allcase:(r + 1) * allcase])
-        return sym(jnp.concatenate(lines, axis=0))
+                rows.append(total[:, r * allcase:(r + 1) * allcase])
+        return sym(jnp.concatenate(rows, axis=0))
 
     def sym(g):
         return 0.5 * (g + g.T)
@@ -363,22 +374,6 @@
         fetch.wait()
     inv_tab = table(jnp.concatenate([binv_ref[t] for t in range(kinds)], axis=1))
     coup_tab = table(jnp.concatenate([coup_ref[t].T for t in range(kinds)], axis=1))
-    def ask():
-        naming = jnp.concatenate(
-            [
-                jnp.where(step_sub == step_row, row, 0.0)
-                for row in ((far_row + 1).astype(F32), kind_row.astype(F32), stiff_ref[...])
-            ],
-            axis=0,
-        )
-        ranked = jnp.where(sub == rank, 1.0, 0.0)
-        wanted = exact(naming, ranked, NT)
-        wanted = jnp.concatenate([wanted[r * parts:(r + 1) * parts] for r in range(3)], axis=1)
-        wanted = wanted.reshape(parts, 1, 3 * ncomp)
-        ask_send[...] = wanted
-        ask_recv[0] = wanted[0]
-        send_parts(lambda i: ask_send.at[i], lambda i: ask_recv.at[i], 0, 1)
-
     ready = [0] + [-(-((j + 1) * width) // pd) for j in range(chunks)]
     condensed_near, leaving = [], None
     for j in range(chunks):
@@ -391,10 +386,22 @@
         out = tall(condensed[pd:], ncomp)
         leaving = out if leaving is None else jnp.concatenate([leaving, out], axis=0)
         if j == 0:
+            naming = jnp.concatenate(
+                [
+                    jnp.where(step_sub == step_row, row, 0.0)
+                    for row in ((far_row + 1).astype(F32), kind_row.astype(F32), stiff_ref[...])
+                ],
+                axis=0,
+            )
+            ranked = jnp.where(sub == rank, 1.0, 0.0)
+            wanted = exact(naming, ranked, NT)
+            wanted = jnp.concatenate([wanted[r * parts:(r + 1) * parts] for r in range(3)], axis=1)
+            wanted = wanted.reshape(parts, 1, 3 * ncomp)
+            ask_send[...] = wanted
+            ask_recv[0] = wanted[0]
             pl.semaphore_wait(barrier, parts + nq - 2)
+            send_parts(lambda i: ask_send.at[i], lambda i: ask_recv.at[i], 0, 1)
         post(0, j, at_slots(slot_pick, part(leaving, j)).reshape(parts, depth, width), 1)
-        if j == 0:
-            ask()
     for fetch in fetches[8:]:
         fetch.wait()
     near_in = jnp.where(sub == near_row, 1.0, 0.0).astype(BF16)
@@ -429,12 +436,14 @@
 
     slot_masks = kind_masks(slot_line(1))
     slot_stiff = tile_cases(slot_line(2))
-    both_picks = jnp.concatenate([asked_pick, near_slots], axis=0)
 
     def scatter(e, j, piece):
-        out = at_slots(both_picks, piece)
-        post(e, j, out[:slots].reshape(parts, depth, width), -1)
-        return lambda: post(e + 1, j, out[slots:].reshape(parts, depth, width), 1)
+        post(e, j, at_slots(asked_pick, piece).reshape(parts, depth, width), -1)
+
+        def rest_of_it():
+            post(e + 1, j, at_slots(near_slots, piece).reshape(parts, depth, width), 1)
+
+        return rest_of_it
 
     def join(a, b):
         return b if a is None else jnp.concatenate([a, b], axis=0)
@@ -459,14 +468,12 @@
     def take_far_values(e, j):
         return place(take(e, j), slot_pick)
 
-    cuts = [0] + [((j + 1) * width) // pd for j in range(chunks)]
-
     base = None
     for j in range(chunks):
         piece = part(own, j) + place(take(0, j), asked_pick)
         scatter(1, j, piece)()
+        publish(0, j, piece)
         base = join(base, piece)
-    publish(0, base)
 
     y_near, y_far = diagonal(1, base)
     far_base, near_at, first, sent, later = None, None, None, 0, []
@@ -474,50 +481,67 @@
         a, b = cuts[j], cuts[j + 1]
         if j == chunks - 1:
             forward(0)
-        far_base = join(far_base, take_far_values(1, j))
+        piece = take_far_values(1, j)
+        publish(3, j, piece)
+        far_base = join(far_base, piece)
         near_at = join(near_at, take(2, j))
         rows = slice(a * pd, b * pd)
         y = y_near[:, a * ncomp:b * ncomp] + near_side(nf_tab, far_base[rows], a, b)
         done = near_ports(y)
         y = y_far[:, a * slots:b * slots] + far_side(fn_tab, near_at[rows], a, b)
-        first = join(first, done + far_ports(y))
+        done = done + far_ports(y)
+        first = join(first, done)
         while (sent + 1) * width <= b * pd:
             later.append(scatter(3, sent, part(first, sent)))
             sent += 1
-    publish(1, first)
+        publish(1, j, done)
 
     y_near, y_far = diagonal(3, first)
     straight = near_ports(y_near) + far_ports(y_far)
     collect(0)
     early = against(jnp.concatenate([own_rows(0), own_rows(1)], axis=0), 0)
+    gram_out(1, early[ncase:])
     gram_out(0, early[:ncase])
-    gram_out(1, early[ncase:])
-    for post_near in later:
-        post_near()
-    publish(3, far_base)
+    forward(3)
+    forward(1)
     far_first, crossed = None, None
     for j in range(chunks):
         a, b = cuts[j], cuts[j + 1]
         if j == chunks - 1:
-            forward(1)
-        far_first = join(far_first, take_far_values(3, j))
+            collect(1)
+            gram_out(2, against(own_rows(1), 1))
+        piece = take_far_values(3, j)
+        far_first = join(far_first, piece)
         crossed = join(crossed, near_ports(near_side(nf_tab, far_first[a * pd:b * pd], a, b)))
-    collect(1)
-    bent = straight + 2.0 * crossed
-    for k in range(ncase):
-        bent_rows[:, k, :] = bent[k * pd:(k + 1) * pd]
-    lines = jnp.concatenate([bent_rows[d] for d in range(pd)], axis=1)
-    late = against(jnp.concatenate([lines, own_rows(1)], axis=0), 1)
-    gram_out(3, late[:ncase])
-    gram_out(2, late[ncase:])
-    publish(4, far_first)
+        if j == 0:
+            for post_near in later:
+                post_near()
+        if j < chunks - 1:
+            publish(4, j, piece)
+    bent_rows[...] = straight + 2.0 * crossed
+    bent = jnp.concatenate([lines(bent_rows, d) for d in range(pd)], axis=1)
+    gram_out(3, against(bent, 1))
+    publish(4, chunks - 1, piece)
+
     n = allcase
-    g00, g01 = gram_in(0), gram_in(1)
     eye = jnp.where(
         lax.broadcasted_iota(jnp.int32, (n, n), 0) == lax.broadcasted_iota(jnp.int32, (n, n), 1),
         1.0,
         0.0,
     )
+    near_at = None
+
+    def finish_second(j, near_at):
+        a, b = cuts[j], cuts[j + 1]
+        rows = slice(a * pd, b * pd)
+        near_at = join(near_at, take(4, j))
+        y = far_side(fn_tab, near_at[rows], a, b)
+        publish(2, j, straight[rows] + crossed[rows] + far_ports(y))
+        return near_at
+
+    for j in range(chunks // 2):
+        near_at = finish_second(j, near_at)
+    g00, g01 = gram_in(0), gram_in(1)
     both = gauss_solve(g01, jnp.concatenate([g00, eye], axis=1))
     mine = jnp.where(
         lax.broadcasted_iota(jnp.int32, (n, ncase), 0)
@@ -527,21 +551,14 @@
     )
     chosen = exact(jnp.concatenate([both[:, 0:n], g01], axis=0), mine)
     first_step, g01_mine, inverse = chosen[0:n], chosen[n:2 * n], both[:, n:2 * n]
-    second, near_at = None, None
-    for j in range(chunks):
-        a, b = cuts[j], cuts[j + 1]
-        if j == chunks - 1:
-            forward(3)
-        near_at = join(near_at, take(4, j))
-        second = join(second, far_ports(far_side(fn_tab, near_at[a * pd:b * pd], a, b)))
-    second = second + straight + crossed
-    publish(2, second)
-
+    for j in range(chunks // 2, chunks):
+        near_at = finish_second(j, near_at)
+    forward(4)
+    collect(3)
     g11 = gram_in(2)
     over = exact(inverse, g11)
     side = exact(g11, jnp.concatenate([over, first_step], axis=1))
-    collect(3)
-    forward(4)
+    collect(4)
     g12 = gram_in(3)
     beta = gauss_solve(g12 - sym(side[:, 0:n]), side[:, n:] - g01_mine)
     alpha = first_step + exact(over, beta)
@@ -557,8 +574,6 @@
     answer_rows = mix(0)
     for d in range(pd):
         sol_ref[d] = answer_rows[:, d * nport:(d + 1) * nport]
-    collect(4)
-    forward(2)
     far_rows = mix(3)
     for d in range(pd):
         nat_far[d] = far_rows[:, d * nport:(d + 1) * nport]
@@ -568,13 +583,14 @@
         [near, jnp.concatenate([nat_far[:, k, :] for k in range(ncase)], axis=1)], axis=0
     )
     scaled = inv_keep[...] / stiff
+    forward(2)
     back = scaled - apply_tables(red_tab, ends, masks)
     for k in range(ncase):
         bub_ref[:, k, :] = back[:, k * ncomp:(k + 1) * ncomp]
     collect(2)
     drop_rows = mix(1)
     for d in range(pd):
-        res_ref[d] = gath[0, my_c, d] - drop_rows[:, d * nport:(d + 1) * nport]
+        res_ref[d] = lines(gath.at[0, my_c], d) - drop_rows[:, d * nport:(d + 1) * nport]
 
     wait_on(far_send.at[:, :, rest], send_sem.at[0])
     wait_on(gath.at[:, pl.ds(1, nq - 1)], send_sem.at[1])
@@ -650,8 +666,8 @@
             pltpu.VMEM((parts, 1, 3 * ncomp), F32),
             pltpu.VMEM((5, chunks, parts, depth, width), F32),
             pltpu.VMEM((5, chunks, parts, depth, width), F32),
-            pltpu.VMEM((5, nq, pd, ncase, nport), F32),
-            pltpu.VMEM((pd, ncase, nport), F32),
+            pltpu.VMEM((5, nq, ncase * pd, nport), F32),
+            pltpu.VMEM((ncase * pd, nport), F32),
             pltpu.VMEM((5 * allcase, pd * nport), BF16),
             pltpu.VMEM((5 * allcase, pd * nport), BF16),
             pltpu.VMEM((4, ncase // fold, fold * allcase), F32),
@@ -661,7 +677,7 @@
             pltpu.SemaphoreType.DMA((10,)),
             pltpu.SemaphoreType.DMA((4,)),
             pltpu.SemaphoreType.DMA((1 + 5 * chunks,)),
-            pltpu.SemaphoreType.DMA((5, nq)),
+            pltpu.SemaphoreType.DMA((5, chunks, nq)),
             pltpu.SemaphoreType.DMA((4,)),
         ],
         compiler_params=pltpu.CompilerParams(

time: 53.8 us -> 53.7 us (level)
  no operation moved by 1% of the time
where the time goes in v7:
time: 53.7 us; the launch traced here: 53.5 us
  Pallas kernels  52.9 us (99%)
  between operations  0.64 us (1%)
    pallas_call x1, Pallas kernels, local(): pl.pallas_call(body, out_shape=shapes, in_specs=[hbm] * 10, out_specs=(vm...  52 us

profile of v7, /device:TPU:0, one launch (start us, length us, event | category | flops | bytes accessed | tf_op | source)
XLA Modules:
  0.0 53.5 jit_solution(10962425396194252994)
XLA Ops:
  0.6 52.0 %condensed_solve.1 = (f32[48,8,128]{2,1,0:T(8,128)S(1)}, f32[48,8,128]{2,1,0:T(8,128)S(1)}, f32[64,8,128]{2,1,0:T(8,128)S(1)}) custom-call(s32[1,128]{1,0:T(1,128)} %bitcast.7, s32[1,128]{1,0:T(1,128)} %bitcast.8, s32[1,128]{1,0:T(1,128)} %bitcast.9, s32[1,128]{1,0:T(1,128)} %bitcast.10, f32[1,128]{1,0:T(1,128)} %bitcast.11, f32[64,8,128]{2,1,0:T(8,128)} %refs_5_.1, ...), custom_call_target="tpu_custom_call" | custom-call | tf_op jit(solution)/shard_map/condensed_solve/pallas_call | solution.py:649
  52.7 0.9 %emit.1 = (f32[48,8,128]{2,1,0:T(8,128)}, f32[48,8,128]{2,1,0:T(8,128)}, f32[64,8,128]{2,1,0:T(8,128)}) custom-call(f32[48,8,128]{2,1,0:T(8,128)S(1)} %get-tuple-element.6.refs_0_, f32[48,8,128]{2,1,0:T(8,128)S(1)} %get-tuple-element.7.refs_1_, f32[64,8,128]{2,1,0:T(8,128)S(1)} %get-tuple-element.8.refs_2_), custom_call_target="tpu_custom_call" | custom-call | tf_op jit(solution)/shard_map/emit/pallas_call | solution.py:704

commit v8 on v7

--- a/solution.py
+++ b/solution.py
@@ -164,7 +164,7 @@
     slots = parts * depth
     allcase = nq * ncase
 
-    for fetch in fetches[0:5]:
+    for fetch in fetches[0:8]:
         fetch.wait()
     kind_row = kind_ref[...]
     near_row = near_ref[...]
@@ -336,7 +336,7 @@
         return jnp.concatenate([lines(gath.at[f, my_c], d) for d in range(pd)], axis=1)
 
     def gram_out(s, block):
-        high = ncase // fold
+        high = block.shape[0] // fold
         folded = jnp.concatenate([block[r * high:(r + 1) * high] for r in range(fold)], axis=1)
         gram_send[s] = folded
         gram_recv[s, my_c * parts] = folded
@@ -357,12 +357,18 @@
 
     def gram_in(s):
         wait_on(gram_recv.at[s, others], gram_rsem.at[s])
-        rows = []
+        blocks = []
         for q in range(nq):
             total = jnp.sum(gram_recv[s, q * parts:(q + 1) * parts], axis=0)
-            for r in range(fold):
-                rows.append(total[:, r * allcase:(r + 1) * allcase])
-        return sym(jnp.concatenate(rows, axis=0))
+            blocks.append(
+                jnp.concatenate(
+                    [total[:, r * allcase:(r + 1) * allcase] for r in range(fold)], axis=0
+                )
+            )
+        return (
+            sym(jnp.concatenate([block[:ncase] for block in blocks], axis=0)),
+            sym(jnp.concatenate([block[ncase:] for block in blocks], axis=0)),
+        )
 
     def sym(g):
         return 0.5 * (g + g.T)
@@ -370,8 +376,6 @@
     def part(x, j):
         return x[j * width:(j + 1) * width]
 
-    for fetch in fetches[5:8]:
-        fetch.wait()
     inv_tab = table(jnp.concatenate([binv_ref[t] for t in range(kinds)], axis=1))
     coup_tab = table(jnp.concatenate([coup_ref[t].T for t in range(kinds)], axis=1))
     ready = [0] + [-(-((j + 1) * width) // pd) for j in range(chunks)]
@@ -499,28 +503,24 @@
     y_near, y_far = diagonal(3, first)
     straight = near_ports(y_near) + far_ports(y_far)
     collect(0)
-    early = against(jnp.concatenate([own_rows(0), own_rows(1)], axis=0), 0)
-    gram_out(1, early[ncase:])
-    gram_out(0, early[:ncase])
-    forward(3)
-    forward(1)
+    gram_out(0, against(jnp.concatenate([own_rows(0), own_rows(1)], axis=0), 0))
     far_first, crossed = None, None
     for j in range(chunks):
         a, b = cuts[j], cuts[j + 1]
         if j == chunks - 1:
+            forward(1)
+            forward(3)
             collect(1)
-            gram_out(2, against(own_rows(1), 1))
         piece = take_far_values(3, j)
         far_first = join(far_first, piece)
         crossed = join(crossed, near_ports(near_side(nf_tab, far_first[a * pd:b * pd], a, b)))
-        if j == 0:
-            for post_near in later:
-                post_near()
         if j < chunks - 1:
+            later[j]()
             publish(4, j, piece)
     bent_rows[...] = straight + 2.0 * crossed
     bent = jnp.concatenate([lines(bent_rows, d) for d in range(pd)], axis=1)
-    gram_out(3, against(bent, 1))
+    gram_out(1, against(jnp.concatenate([own_rows(1), bent], axis=0), 1))
+    later[chunks - 1]()
     publish(4, chunks - 1, piece)
 
     n = allcase
@@ -539,9 +539,7 @@
         publish(2, j, straight[rows] + crossed[rows] + far_ports(y))
         return near_at
 
-    for j in range(chunks // 2):
-        near_at = finish_second(j, near_at)
-    g00, g01 = gram_in(0), gram_in(1)
+    g00, g01 = gram_in(0)
     both = gauss_solve(g01, jnp.concatenate([g00, eye], axis=1))
     mine = jnp.where(
         lax.broadcasted_iota(jnp.int32, (n, ncase), 0)
@@ -551,15 +549,13 @@
     )
     chosen = exact(jnp.concatenate([both[:, 0:n], g01], axis=0), mine)
     first_step, g01_mine, inverse = chosen[0:n], chosen[n:2 * n], both[:, n:2 * n]
-    for j in range(chunks // 2, chunks):
+    for j in range(chunks):
         near_at = finish_second(j, near_at)
     forward(4)
     collect(3)
-    g11 = gram_in(2)
+    g11, g12 = gram_in(1)
     over = exact(inverse, g11)
     side = exact(g11, jnp.concatenate([over, first_step], axis=1))
-    collect(4)
-    g12 = gram_in(3)
     beta = gauss_solve(g12 - sym(side[:, 0:n]), side[:, n:] - g01_mine)
     alpha = first_step + exact(over, beta)
     coefs = jnp.concatenate([alpha, -beta], axis=0).T
@@ -574,7 +570,9 @@
     answer_rows = mix(0)
     for d in range(pd):
         sol_ref[d] = answer_rows[:, d * nport:(d + 1) * nport]
+    collect(4)
     far_rows = mix(3)
+    forward(2)
     for d in range(pd):
         nat_far[d] = far_rows[:, d * nport:(d + 1) * nport]
     answer = jnp.concatenate([sol_ref[:, k, :] for k in range(ncase)], axis=0)
@@ -583,7 +581,6 @@
         [near, jnp.concatenate([nat_far[:, k, :] for k in range(ncase)], axis=1)], axis=0
     )
     scaled = inv_keep[...] / stiff
-    forward(2)
     back = scaled - apply_tables(red_tab, ends, masks)
     for k in range(ncase):
         bub_ref[:, k, :] = back[:, k * ncomp:(k + 1) * ncomp]
@@ -670,15 +667,15 @@
             pltpu.VMEM((ncase * pd, nport), F32),
             pltpu.VMEM((5 * allcase, pd * nport), BF16),
             pltpu.VMEM((5 * allcase, pd * nport), BF16),
-            pltpu.VMEM((4, ncase // fold, fold * allcase), F32),
-            pltpu.VMEM((4, nq * parts, ncase // fold, fold * allcase), F32),
+            pltpu.VMEM((2, 2 * ncase // fold, fold * allcase), F32),
+            pltpu.VMEM((2, nq * parts, 2 * ncase // fold, fold * allcase), F32),
             pltpu.VMEM((modes, ncase * ncomp), F32),
             pltpu.VMEM((pd, ncase, nport), F32),
             pltpu.SemaphoreType.DMA((10,)),
             pltpu.SemaphoreType.DMA((4,)),
             pltpu.SemaphoreType.DMA((1 + 5 * chunks,)),
             pltpu.SemaphoreType.DMA((5, chunks, nq)),
-            pltpu.SemaphoreType.DMA((4,)),
+            pltpu.SemaphoreType.DMA((2,)),
         ],
         compiler_params=pltpu.CompilerParams(
             collective_id=0, has_side_effects=True, vmem_limit_bytes=32 * 1024 * 1024

time: 53.7 us -> 52.5 us (0.978)
  Pallas kernels: 52.9 us -> 51.6 us
    pallas_call x1, Pallas kernels: 52 us -> 50.8 us  [local(): pl.pallas_call(body, out_shape=shapes, in_specs=[hbm] * 10, out_specs=(vm...]
where the time goes in v8:
time: 52.5 us; the launch traced here: 52.3 us
  Pallas kernels  51.6 us (98%)
  between operations  0.64 us (1%)
    pallas_call x1, Pallas kernels, local(): pl.pallas_call(body, out_shape=shapes, in_specs=[hbm] * 10, out_specs=(vm...  50.8 us

profile of v8, /device:TPU:0, one launch (start us, length us, event | category | flops | bytes accessed | tf_op | source)
XLA Modules:
  0.0 52.3 jit_solution(8670761863585226751)
XLA Ops:
  0.6 50.8 %condensed_solve.1 = (f32[48,8,128]{2,1,0:T(8,128)S(1)}, f32[48,8,128]{2,1,0:T(8,128)S(1)}, f32[64,8,128]{2,1,0:T(8,128)S(1)}) custom-call(s32[1,128]{1,0:T(1,128)} %bitcast.7, s32[1,128]{1,0:T(1,128)} %bitcast.8, s32[1,128]{1,0:T(1,128)} %bitcast.9, s32[1,128]{1,0:T(1,128)} %bitcast.10, f32[1,128]{1,0:T(1,128)} %bitcast.11, f32[64,8,128]{2,1,0:T(8,128)} %refs_5_.1, ...), custom_call_target="tpu_custom_call" | custom-call | tf_op jit(solution)/shard_map/condensed_solve/pallas_call | solution.py:646
  51.4 0.9 %emit.1 = (f32[48,8,128]{2,1,0:T(8,128)}, f32[48,8,128]{2,1,0:T(8,128)}, f32[64,8,128]{2,1,0:T(8,128)}) custom-call(f32[48,8,128]{2,1,0:T(8,128)S(1)} %get-tuple-element.6.refs_0_, f32[48,8,128]{2,1,0:T(8,128)S(1)} %get-tuple-element.7.refs_1_, f32[64,8,128]{2,1,0:T(8,128)S(1)} %get-tuple-element.8.refs_2_), custom_call_target="tpu_custom_call" | custom-call | tf_op jit(solution)/shard_map/emit/pallas_call | solution.py:701

commit v9 on v8

--- a/solution.py
+++ b/solution.py
@@ -164,7 +164,7 @@
     slots = parts * depth
     allcase = nq * ncase
 
-    for fetch in fetches[0:8]:
+    for fetch in fetches[0:5]:
         fetch.wait()
     kind_row = kind_ref[...]
     near_row = near_ref[...]
@@ -273,12 +273,12 @@
             return pl.ds(cuts[j] * pd, (cuts[j + 1] - cuts[j]) * pd)
         return pl.ds(j * width, width)
 
-    def send_case(f, j, block, sem, step):
+    def send_case(f, block, sem, step):
         pltpu.make_async_remote_copy(
             src_ref=block,
             dst_ref=block,
             send_sem=send_sem.at[1],
-            recv_sem=case_rsem.at[f, j, sem],
+            recv_sem=case_rsem.at[f, sem - 1],
             device_id=case_id(step),
             device_id_type=MESH,
         ).start()
@@ -286,14 +286,13 @@
     def publish(f, j, rows):
         gath[f, my_c, span(f, j)] = rows
         for i in reversed(direct):
-            send_case(f, j, gath.at[f, my_c, span(f, j)], i, i)
-
-    def forward(f, *pieces):
+            send_case(f, gath.at[f, my_c, span(f, j)], i, i)
+
+    def forward(f):
         if nq == 4:
-            for j in pieces or range(chunks):
-                block = gath.at[f, case_from(2), span(f, j)]
-                wait_on(block, case_rsem.at[f, j, 2])
-                send_case(f, j, block, 3, 1)
+            block = gath.at[f, case_from(2)]
+            wait_on(block, case_rsem.at[f, 1])
+            send_case(f, block, 3, 1)
 
     def lines(ref, d):
         return ref[pl.ds(d, ncase, stride=pd), :]
@@ -301,8 +300,7 @@
     def collect(f):
         for i in range(1, nq):
             if nq != 4 or i != 2:
-                for j in range(chunks):
-                    wait_on(gath.at[f, case_from(i), span(f, j)], case_rsem.at[f, j, i])
+                wait_on(gath.at[f, case_from(i)], case_rsem.at[f, i - 1])
 
         def body(d, _):
             cols = pl.ds(pl.multiple_of(d * nport, nport), nport)
@@ -312,7 +310,7 @@
             rows_low[f * allcase:(f + 1) * allcase, cols] = low
             return 0
 
-        lax.fori_loop(0, pd, body, 0, unroll=4)
+        lax.fori_loop(0, pd, body, 0, unroll=16)
 
     def against(x, f):
         top, low = split(x)
@@ -376,6 +374,8 @@
     def part(x, j):
         return x[j * width:(j + 1) * width]
 
+    for fetch in fetches[5:8]:
+        fetch.wait()
     inv_tab = table(jnp.concatenate([binv_ref[t] for t in range(kinds)], axis=1))
     coup_tab = table(jnp.concatenate([coup_ref[t].T for t in range(kinds)], axis=1))
     ready = [0] + [-(-((j + 1) * width) // pd) for j in range(chunks)]
@@ -511,6 +511,7 @@
             forward(1)
             forward(3)
             collect(1)
+            square = against(own_rows(1), 1)
         piece = take_far_values(3, j)
         far_first = join(far_first, piece)
         crossed = join(crossed, near_ports(near_side(nf_tab, far_first[a * pd:b * pd], a, b)))
@@ -519,7 +520,7 @@
             publish(4, j, piece)
     bent_rows[...] = straight + 2.0 * crossed
     bent = jnp.concatenate([lines(bent_rows, d) for d in range(pd)], axis=1)
-    gram_out(1, against(jnp.concatenate([own_rows(1), bent], axis=0), 1))
+    gram_out(1, jnp.concatenate([square, against(bent, 1)], axis=0))
     later[chunks - 1]()
     publish(4, chunks - 1, piece)
 
@@ -550,9 +551,10 @@
     chosen = exact(jnp.concatenate([both[:, 0:n], g01], axis=0), mine)
     first_step, g01_mine, inverse = chosen[0:n], chosen[n:2 * n], both[:, n:2 * n]
     for j in range(chunks):
+        if j == chunks - 1:
+            collect(3)
         near_at = finish_second(j, near_at)
     forward(4)
-    collect(3)
     g11, g12 = gram_in(1)
     over = exact(inverse, g11)
     side = exact(g11, jnp.concatenate([over, first_step], axis=1))
@@ -572,7 +574,6 @@
         sol_ref[d] = answer_rows[:, d * nport:(d + 1) * nport]
     collect(4)
     far_rows = mix(3)
-    forward(2)
     for d in range(pd):
         nat_far[d] = far_rows[:, d * nport:(d + 1) * nport]
     answer = jnp.concatenate([sol_ref[:, k, :] for k in range(ncase)], axis=0)
@@ -581,6 +582,7 @@
         [near, jnp.concatenate([nat_far[:, k, :] for k in range(ncase)], axis=1)], axis=0
     )
     scaled = inv_keep[...] / stiff
+    forward(2)
     back = scaled - apply_tables(red_tab, ends, masks)
     for k in range(ncase):
         bub_ref[:, k, :] = back[:, k * ncomp:(k + 1) * ncomp]
@@ -674,7 +676,7 @@
             pltpu.SemaphoreType.DMA((10,)),
             pltpu.SemaphoreType.DMA((4,)),
             pltpu.SemaphoreType.DMA((1 + 5 * chunks,)),
-            pltpu.SemaphoreType.DMA((5, chunks, nq)),
+            pltpu.SemaphoreType.DMA((5, nq - 1)),
             pltpu.SemaphoreType.DMA((2,)),
         ],
         compiler_params=pltpu.CompilerParams(

time: 52.5 us -> 52.6 us (level); the launches traced: 52.3 us -> 51.8 us
  Pallas kernels: 51.6 us -> 51 us
    pallas_call x1, Pallas kernels: 50.8 us -> 50.2 us  [local(): pl.pallas_call(body, out_shape=shapes, in_specs=[hbm] * 10, out_specs=(vm...]
where the time goes in v9:
time: 52.6 us; the launch traced here: 51.8 us
  Pallas kernels  51 us (97%)
  between operations  0.8 us (2%)
    pallas_call x1, Pallas kernels, local(): pl.pallas_call(body, out_shape=shapes, in_specs=[hbm] * 10, out_specs=(vm...  50.2 us

profile of v9, /device:TPU:0, one launch (start us, length us, event | category | flops | bytes accessed | tf_op | source)
XLA Modules:
  0.0 51.8 jit_solution(13752919194932594968)
XLA Ops:
  0.6 50.2 %condensed_solve.1 = (f32[48,8,128]{2,1,0:T(8,128)S(1)}, f32[48,8,128]{2,1,0:T(8,128)S(1)}, f32[64,8,128]{2,1,0:T(8,128)S(1)}) custom-call(s32[1,128]{1,0:T(1,128)} %bitcast.7, s32[1,128]{1,0:T(1,128)} %bitcast.8, s32[1,128]{1,0:T(1,128)} %bitcast.9, s32[1,128]{1,0:T(1,128)} %bitcast.10, f32[1,128]{1,0:T(1,128)} %bitcast.11, f32[64,8,128]{2,1,0:T(8,128)} %refs_5_.1, ...), custom_call_target="tpu_custom_call" | custom-call | tf_op jit(solution)/shard_map/condensed_solve/pallas_call | solution.py:648
  50.8 0.9 %emit.1 = (f32[48,8,128]{2,1,0:T(8,128)}, f32[48,8,128]{2,1,0:T(8,128)}, f32[64,8,128]{2,1,0:T(8,128)}) custom-call(f32[48,8,128]{2,1,0:T(8,128)S(1)} %get-tuple-element.6.refs_0_, f32[48,8,128]{2,1,0:T(8,128)S(1)} %get-tuple-element.7.refs_1_, f32[64,8,128]{2,1,0:T(8,128)S(1)} %get-tuple-element.8.refs_2_), custom_call_target="tpu_custom_call" | custom-call | tf_op jit(solution)/shard_map/emit/pallas_call | solution.py:703

commit v10 on v7

--- a/solution.py
+++ b/solution.py
@@ -26,22 +26,43 @@
     return lax.dot_general(a, b, dims, precision=HIGH, preferred_element_type=F32)
 
 
-def gauss_solve(matrix, target):
+def invert(a, b, c, d):
+    scale = 1.0 / (a * d - b * c)
+    return d * scale, -b * scale, -c * scale, a * scale
+
+
+def times(m, x):
+    return m[0] * x[0] + m[1] * x[1], m[2] * x[0] + m[3] * x[1]
+
+
+def gauss_solve(matrix, target, gain):
     n = matrix.shape[0]
-    aug = jnp.concatenate([matrix, target], axis=1)
+    gain_row, gain_col = gain
+    aug = jnp.concatenate([matrix * gain_row, target], axis=1) * gain_col
     rows = lax.broadcasted_iota(jnp.int32, aug.shape, 0)
-    for j in range(0, n, 2):
-        row0, row1 = aug[j:j + 1, :], aug[j + 1:j + 2, :]
-        col0 = jnp.broadcast_to(aug[:, j:j + 1], aug.shape)
-        col1 = jnp.broadcast_to(aug[:, j + 1:j + 2], aug.shape)
-        a, c = col0[j:j + 1, :], col0[j + 1:j + 2, :]
-        b, d = col1[j:j + 1, :], col1[j + 1:j + 2, :]
-        scale = 1.0 / (a * d - b * c)
-        new0 = (d * row0 - b * row1) * scale
-        new1 = (a * row1 - c * row0) * scale
-        rest = aug - col0 * new0 - col1 * new1
-        aug = jnp.where(rows == j, new0, jnp.where(rows == j + 1, new1, rest))
-    return aug[:, n:]
+    for j in range(0, n, 4):
+        cols = [jnp.broadcast_to(aug[:, j + k:j + k + 1], aug.shape) for k in range(4)]
+        line = [aug[j + k:j + k + 1, :] for k in range(4)]
+        p = [[cols[k][j + i:j + i + 1, :] for k in range(4)] for i in range(4)]
+        lead = invert(p[0][0], p[0][1], p[1][0], p[1][1])
+        left, right = times(lead, (p[0][2], p[1][2])), times(lead, (p[0][3], p[1][3]))
+        low = (p[2][0], p[2][1], p[3][0], p[3][1])
+        under_left, under_right = times(low, left), times(low, right)
+        tail = invert(
+            p[2][2] - under_left[0],
+            p[2][3] - under_right[0],
+            p[3][2] - under_left[1],
+            p[3][3] - under_right[1],
+        )
+        top = times(lead, (line[0], line[1]))
+        carried = times(low, top)
+        new2, new3 = times(tail, (line[2] - carried[0], line[3] - carried[1]))
+        new0 = top[0] - left[0] * new2 - right[0] * new3
+        new1 = top[1] - left[1] * new2 - right[1] * new3
+        aug = (aug - cols[0] * new0 - cols[1] * new1) - (cols[2] * new2 + cols[3] * new3)
+        for k, new in enumerate((new0, new1, new2, new3)):
+            aug = jnp.where(rows == j + k, new, aug)
+    return aug[:, n:] * gain_col
 
 
 def kernel(
@@ -112,6 +133,14 @@
     barrier = pltpu.get_barrier_semaphore()
 
     order = sorted(range(1, parts), key=lambda i: -min(i % npy, npy - i % npy))
+    if npy == 4 and parts == 2 * npy:
+        half = my_y // 2
+        rows = (3 - 3 * half, 2 - half, my_y + 1 - 2 * lax.rem(my_y, 2), my_y)
+        order = [
+            lax.rem(x * npy + y - me + parts, parts)
+            for y in rows
+            for x in ((1 - my_x, my_x) if y is not my_y else (1 - my_x,))
+        ]
 
     def each_other(act):
         def per_part(i, _):
@@ -197,7 +226,7 @@
 
         if parts <= 8:
             for i in order:
-                body(i, 0)
+                body(i if sign > 0 else parts - i, 0)
         else:
             lax.fori_loop(1, parts, body, 0)
 
@@ -273,27 +302,37 @@
             return pl.ds(cuts[j] * pd, (cuts[j + 1] - cuts[j]) * pd)
         return pl.ds(j * width, width)
 
-    def send_case(f, j, block, sem, step):
+    lanes_of = {f: (f,) for f in range(5)}
+    if chunks > 1:
+        lanes_of[2] = (2, 5)
+
+    def lane_span(lane):
+        if lane == 5:
+            return span(2, chunks - 1)
+        return pl.ds(0, cuts[chunks - 1] * pd if lane == 2 and chunks > 1 else ncase * pd)
+
+    def send_case(lane, block, sem, step):
         pltpu.make_async_remote_copy(
             src_ref=block,
             dst_ref=block,
             send_sem=send_sem.at[1],
-            recv_sem=case_rsem.at[f, j, sem],
+            recv_sem=case_rsem.at[lane, sem - 1],
             device_id=case_id(step),
             device_id_type=MESH,
         ).start()
 
     def publish(f, j, rows):
         gath[f, my_c, span(f, j)] = rows
+        lane = lanes_of[f][-1] if j == chunks - 1 else f
         for i in reversed(direct):
-            send_case(f, j, gath.at[f, my_c, span(f, j)], i, i)
-
-    def forward(f, *pieces):
+            send_case(lane, gath.at[f, my_c, span(f, j)], i, i)
+
+    def forward(f, *lanes):
         if nq == 4:
-            for j in pieces or range(chunks):
-                block = gath.at[f, case_from(2), span(f, j)]
-                wait_on(block, case_rsem.at[f, j, 2])
-                send_case(f, j, block, 3, 1)
+            for lane in lanes or lanes_of[f]:
+                block = gath.at[f, case_from(2), lane_span(lane)]
+                wait_on(block, case_rsem.at[lane, 1])
+                send_case(lane, block, 3, 1)
 
     def lines(ref, d):
         return ref[pl.ds(d, ncase, stride=pd), :]
@@ -301,8 +340,8 @@
     def collect(f):
         for i in range(1, nq):
             if nq != 4 or i != 2:
-                for j in range(chunks):
-                    wait_on(gath.at[f, case_from(i), span(f, j)], case_rsem.at[f, j, i])
+                for lane in lanes_of[f]:
+                    wait_on(gath.at[f, case_from(i), lane_span(lane)], case_rsem.at[lane, i - 1])
 
         def body(d, _):
             cols = pl.ds(pl.multiple_of(d * nport, nport), nport)
@@ -312,7 +351,7 @@
             rows_low[f * allcase:(f + 1) * allcase, cols] = low
             return 0
 
-        lax.fori_loop(0, pd, body, 0, unroll=4)
+        lax.fori_loop(0, pd, body, 0, unroll=16)
 
     def against(x, f):
         top, low = split(x)
@@ -502,26 +541,24 @@
     early = against(jnp.concatenate([own_rows(0), own_rows(1)], axis=0), 0)
     gram_out(1, early[ncase:])
     gram_out(0, early[:ncase])
-    forward(3)
-    forward(1)
     far_first, crossed = None, None
     for j in range(chunks):
         a, b = cuts[j], cuts[j + 1]
         if j == chunks - 1:
+            forward(1)
+            forward(3)
             collect(1)
             gram_out(2, against(own_rows(1), 1))
         piece = take_far_values(3, j)
+        publish(4, j, piece)
         far_first = join(far_first, piece)
         crossed = join(crossed, near_ports(near_side(nf_tab, far_first[a * pd:b * pd], a, b)))
-        if j == 0:
-            for post_near in later:
-                post_near()
         if j < chunks - 1:
-            publish(4, j, piece)
+            later[j]()
     bent_rows[...] = straight + 2.0 * crossed
     bent = jnp.concatenate([lines(bent_rows, d) for d in range(pd)], axis=1)
     gram_out(3, against(bent, 1))
-    publish(4, chunks - 1, piece)
+    later[chunks - 1]()
 
     n = allcase
     eye = jnp.where(
@@ -539,10 +576,13 @@
         publish(2, j, straight[rows] + crossed[rows] + far_ports(y))
         return near_at
 
-    for j in range(chunks // 2):
-        near_at = finish_second(j, near_at)
-    g00, g01 = gram_in(0), gram_in(1)
-    both = gauss_solve(g01, jnp.concatenate([g00, eye], axis=1))
+    g01, g00 = gram_in(1), gram_in(0)
+
+    def gains(g):
+        diagonal = g * eye
+        return tuple(lax.rsqrt(jnp.sum(diagonal, axis=k, keepdims=True)) for k in (0, 1))
+
+    both = gauss_solve(g01, jnp.concatenate([g00, eye], axis=1), gains(g01))
     mine = jnp.where(
         lax.broadcasted_iota(jnp.int32, (n, ncase), 0)
         == lax.broadcasted_iota(jnp.int32, (n, ncase), 1) + my_c * ncase,
@@ -551,16 +591,16 @@
     )
     chosen = exact(jnp.concatenate([both[:, 0:n], g01], axis=0), mine)
     first_step, g01_mine, inverse = chosen[0:n], chosen[n:2 * n], both[:, n:2 * n]
-    for j in range(chunks // 2, chunks):
+    for j in range(chunks):
+        if j == chunks - 1:
+            collect(3)
+            g11 = gram_in(2)
+            over = exact(inverse, g11)
+            side = exact(g11, jnp.concatenate([over, first_step], axis=1))
         near_at = finish_second(j, near_at)
     forward(4)
-    collect(3)
-    g11 = gram_in(2)
-    over = exact(inverse, g11)
-    side = exact(g11, jnp.concatenate([over, first_step], axis=1))
-    collect(4)
     g12 = gram_in(3)
-    beta = gauss_solve(g12 - sym(side[:, 0:n]), side[:, n:] - g01_mine)
+    beta = gauss_solve(g12 - sym(side[:, 0:n]), side[:, n:] - g01_mine, gains(g12))
     alpha = first_step + exact(over, beta)
     coefs = jnp.concatenate([alpha, -beta], axis=0).T
     ctop, clow = split(coefs)
@@ -574,6 +614,9 @@
     answer_rows = mix(0)
     for d in range(pd):
         sol_ref[d] = answer_rows[:, d * nport:(d + 1) * nport]
+    collect(4)
+    if chunks > 1:
+        forward(2, 2)
     far_rows = mix(3)
     for d in range(pd):
         nat_far[d] = far_rows[:, d * nport:(d + 1) * nport]
@@ -583,7 +626,7 @@
         [near, jnp.concatenate([nat_far[:, k, :] for k in range(ncase)], axis=1)], axis=0
     )
     scaled = inv_keep[...] / stiff
-    forward(2)
+    forward(2, lanes_of[2][-1])
     back = scaled - apply_tables(red_tab, ends, masks)
     for k in range(ncase):
         bub_ref[:, k, :] = back[:, k * ncomp:(k + 1) * ncomp]
@@ -677,7 +720,7 @@
             pltpu.SemaphoreType.DMA((10,)),
             pltpu.SemaphoreType.DMA((4,)),
             pltpu.SemaphoreType.DMA((1 + 5 * chunks,)),
-            pltpu.SemaphoreType.DMA((5, chunks, nq)),
+            pltpu.SemaphoreType.DMA((6, nq - 1)),
             pltpu.SemaphoreType.DMA((4,)),
         ],
         compiler_params=pltpu.CompilerParams(

time: 53.7 us -> 52.3 us (0.974)
  Pallas kernels: 52.9 us -> 50.8 us
    pallas_call x1, Pallas kernels: 52 us -> 50 us  [local(): pl.pallas_call(body, out_shape=shapes, in_specs=[hbm] * 10, out_specs=(vm...]
where the time goes in v10:
time: 52.3 us; the launch traced here: 51.6 us
  Pallas kernels  50.8 us (97%)
  between operations  0.8 us (2%)
    pallas_call x1, Pallas kernels, local(): pl.pallas_call(body, out_shape=shapes, in_specs=[hbm] * 10, out_specs=(vm...  50 us

profile of v10, /device:TPU:0, one launch (start us, length us, event | category | flops | bytes accessed | tf_op | source)
XLA Modules:
  0.0 51.6 jit_solution(10740444236625511749)
XLA Ops:
  0.6 50.0 %condensed_solve.1 = (f32[48,8,128]{2,1,0:T(8,128)S(1)}, f32[48,8,128]{2,1,0:T(8,128)S(1)}, f32[64,8,128]{2,1,0:T(8,128)S(1)}) custom-call(s32[1,128]{1,0:T(1,128)} %bitcast.7, s32[1,128]{1,0:T(1,128)} %bitcast.8, s32[1,128]{1,0:T(1,128)} %bitcast.9, s32[1,128]{1,0:T(1,128)} %bitcast.10, f32[1,128]{1,0:T(1,128)} %bitcast.11, f32[64,8,128]{2,1,0:T(8,128)} %refs_5_.1, ...), custom_call_target="tpu_custom_call" | custom-call | tf_op jit(solution)/shard_map/condensed_solve/pallas_call | solution.py:692
  50.6 0.9 %emit.1 = (f32[48,8,128]{2,1,0:T(8,128)}, f32[48,8,128]{2,1,0:T(8,128)}, f32[64,8,128]{2,1,0:T(8,128)}) custom-call(f32[48,8,128]{2,1,0:T(8,128)S(1)} %get-tuple-element.6.refs_0_, f32[48,8,128]{2,1,0:T(8,128)S(1)} %get-tuple-element.7.refs_1_, f32[64,8,128]{2,1,0:T(8,128)S(1)} %get-tuple-element.8.refs_2_), custom_call_target="tpu_custom_call" | custom-call | tf_op jit(solution)/shard_map/emit/pallas_call | solution.py:747

commit v11 on v10

--- a/solution.py
+++ b/solution.py
@@ -606,10 +606,11 @@
     ctop, clow = split(coefs)
     stack = jnp.concatenate([ctop, clow], axis=0)
 
-    def mix(f):
-        band = slice(f * allcase, (f + 2) * allcase)
-        lead = mm(stack, rows_top[band, :])
-        return lead[0:ncase] + lead[ncase:] + mm(ctop, rows_low[band, :])
+    def mix(f, low=0, high=2):
+        band = slice((f + low) * allcase, (f + high) * allcase)
+        cols = slice(low * allcase, high * allcase)
+        lead = mm(stack[:, cols], rows_top[band, :])
+        return lead[0:ncase] + lead[ncase:] + mm(ctop[:, cols], rows_low[band, :])
 
     answer_rows = mix(0)
     for d in range(pd):
@@ -627,13 +628,16 @@
     )
     scaled = inv_keep[...] / stiff
     forward(2, lanes_of[2][-1])
+    settled = mix(1, 0, 1)
+    for d in range(pd):
+        res_ref[d] = lines(gath.at[0, my_c], d) - settled[:, d * nport:(d + 1) * nport]
     back = scaled - apply_tables(red_tab, ends, masks)
     for k in range(ncase):
         bub_ref[:, k, :] = back[:, k * ncomp:(k + 1) * ncomp]
     collect(2)
-    drop_rows = mix(1)
+    drop_rows = mix(1, 1, 2)
     for d in range(pd):
-        res_ref[d] = lines(gath.at[0, my_c], d) - drop_rows[:, d * nport:(d + 1) * nport]
+        res_ref[d] = res_ref[d] - drop_rows[:, d * nport:(d + 1) * nport]
 
     wait_on(far_send.at[:, :, rest], send_sem.at[0])
     wait_on(gath.at[:, pl.ds(1, nq - 1)], send_sem.at[1])

time: 52.3 us -> 51.8 us (level); the launches traced: 51.6 us -> 51.7 us
  no operation moved by 1% of the time
where the time goes in v11:
time: 51.8 us; the launch traced here: 51.7 us
  Pallas kernels  50.9 us (98%)
  between operations  0.8 us (2%)
    pallas_call x1, Pallas kernels, local(): pl.pallas_call(body, out_shape=shapes, in_specs=[hbm] * 10, out_specs=(vm...  50 us

profile of v11, /device:TPU:0, one launch (start us, length us, event | category | flops | bytes accessed | tf_op | source)
XLA Modules:
  0.0 51.7 jit_solution(17082864335607923799)
XLA Ops:
  0.6 50.0 %condensed_solve.1 = (f32[48,8,128]{2,1,0:T(8,128)S(1)}, f32[48,8,128]{2,1,0:T(8,128)S(1)}, f32[64,8,128]{2,1,0:T(8,128)S(1)}) custom-call(s32[1,128]{1,0:T(1,128)} %bitcast.7, s32[1,128]{1,0:T(1,128)} %bitcast.8, s32[1,128]{1,0:T(1,128)} %bitcast.9, s32[1,128]{1,0:T(1,128)} %bitcast.10, f32[1,128]{1,0:T(1,128)} %bitcast.11, f32[64,8,128]{2,1,0:T(8,128)} %refs_5_.1, ...), custom_call_target="tpu_custom_call" | custom-call | tf_op jit(solution)/shard_map/condensed_solve/pallas_call | solution.py:696
  50.7 0.9 %emit.1 = (f32[48,8,128]{2,1,0:T(8,128)}, f32[48,8,128]{2,1,0:T(8,128)}, f32[64,8,128]{2,1,0:T(8,128)}) custom-call(f32[48,8,128]{2,1,0:T(8,128)S(1)} %get-tuple-element.6.refs_0_, f32[48,8,128]{2,1,0:T(8,128)S(1)} %get-tuple-element.7.refs_1_, f32[64,8,128]{2,1,0:T(8,128)S(1)} %get-tuple-element.8.refs_2_), custom_call_target="tpu_custom_call" | custom-call | tf_op jit(solution)/shard_map/emit/pallas_call | solution.py:751

commit v12 on v11

--- a/solution.py
+++ b/solution.py
@@ -615,9 +615,9 @@
     answer_rows = mix(0)
     for d in range(pd):
         sol_ref[d] = answer_rows[:, d * nport:(d + 1) * nport]
-    collect(4)
     if chunks > 1:
         forward(2, 2)
+    collect(4)
     far_rows = mix(3)
     for d in range(pd):
         nat_far[d] = far_rows[:, d * nport:(d + 1) * nport]

time: 51.8 us -> 51.8 us (level)
  no operation moved by 1% of the time
where the time goes in v12:
time: 51.8 us; the launch traced here: 51.7 us
  Pallas kernels  50.9 us (98%)
  between operations  0.8 us (2%)
    pallas_call x1, Pallas kernels, local(): pl.pallas_call(body, out_shape=shapes, in_specs=[hbm] * 10, out_specs=(vm...  50 us

profile of v12, /device:TPU:0, one launch (start us, length us, event | category | flops | bytes accessed | tf_op | source)
XLA Modules:
  0.0 51.7 jit_solution(2828169263107711338)
XLA Ops:
  0.6 50.0 %condensed_solve.1 = (f32[48,8,128]{2,1,0:T(8,128)S(1)}, f32[48,8,128]{2,1,0:T(8,128)S(1)}, f32[64,8,128]{2,1,0:T(8,128)S(1)}) custom-call(s32[1,128]{1,0:T(1,128)} %bitcast.7, s32[1,128]{1,0:T(1,128)} %bitcast.8, s32[1,128]{1,0:T(1,128)} %bitcast.9, s32[1,128]{1,0:T(1,128)} %bitcast.10, f32[1,128]{1,0:T(1,128)} %bitcast.11, f32[64,8,128]{2,1,0:T(8,128)} %refs_5_.1, ...), custom_call_target="tpu_custom_call" | custom-call | tf_op jit(solution)/shard_map/condensed_solve/pallas_call | solution.py:696
  50.7 0.9 %emit.1 = (f32[48,8,128]{2,1,0:T(8,128)}, f32[48,8,128]{2,1,0:T(8,128)}, f32[64,8,128]{2,1,0:T(8,128)}) custom-call(f32[48,8,128]{2,1,0:T(8,128)S(1)} %get-tuple-element.6.refs_0_, f32[48,8,128]{2,1,0:T(8,128)S(1)} %get-tuple-element.7.refs_1_, f32[64,8,128]{2,1,0:T(8,128)S(1)} %get-tuple-element.8.refs_2_), custom_call_target="tpu_custom_call" | custom-call | tf_op jit(solution)/shard_map/emit/pallas_call | solution.py:751
